TPU v7x, 128 devices: a whole 4x4x4 slice. The times are simulated.
128 devices in a mesh: prow: 8 (over y, core), pcol: 16 (over x, z).
Axes of the slice: x: 4, y: 4, z: 4, core: 2. Of those that a mesh axis runs over, the one named last changes fastest.
Arguments:
- diag_block: float32 [512, 512], P(('prow', 'pcol')), as said below
- panel: float32 [4, 4096, 512], P(None, ('prow', 'pcol')), may hold values from -2.4 to 2.4
- trailing: float32 [4, 4096, 2, 8192], P(None, 'prow', None, 'pcol'), may hold values from -6 to 6
Outputs:
- factor_diag: float32 [512, 512], P(('prow', 'pcol'))
- factor_panel: float32 [4, 4096, 512], P(None, ('prow', 'pcol'))
- updated: float32 [4, 4096, 2, 8192], P(None, 'prow', None, 'pcol')
Inputs may be any that keep to these rules, and one draw needn't show every extreme that they name: diag_block is symmetric positive definite with eigenvalues of at least 1.
All inputs are finite; a program needn't handle non-finite values.
Results may differ from a plain program's by a relative error of at most 0.0003.
Values sent between devices are 32-bit elements; how exact they have to be, the bound alone decides.
A program may use at most 128 MiB of HBM per device.

v0:
```python
import jax
import jax.numpy as jnp
from jax import lax
from jax.sharding import Mesh
from jax.sharding import PartitionSpec as P

PROW = ("prow_0", "prow_1")
PCOL = ("pcol_0", "pcol_1")
PROW_PCOL = ("prow_0", "prow_1", "pcol_0", "pcol_1")


def in_order(blocks, dim):
    blocks = jnp.moveaxis(blocks, 0, dim)
    dims = blocks.shape
    return blocks.reshape(*dims[:dim], dims[dim] * dims[dim + 1], *dims[dim + 2 :])


def stacked_from(value, axes, turns):
    blocks = value
    for k in turns:
        blocks = lax.all_gather(blocks, axes[k])
    done = turns[::-1]
    back = [done.index(k) for k in range(len(axes))]
    blocks = blocks.transpose(*back, *range(len(axes), blocks.ndim))
    return blocks.reshape(-1, *value.shape)


def gather_axes(value, axes, turns, dim):
    return in_order(stacked_from(value, axes, turns), dim)


def padded_to(lines, peers):
    spare = -lines.shape[0] % peers
    if not spare:
        return lines
    return jnp.concatenate([lines, jnp.zeros((spare, *lines.shape[1:]), lines.dtype)])


def spread(value, axis, root):
    lines = jnp.where(lax.axis_index(axis) == root, value, jnp.zeros_like(value)).reshape(
        -1, *value.shape[1:][-1:]
    )
    padded = padded_to(lines, lax.axis_size(axis))
    own = lax.psum_scatter(padded, axis, scatter_dimension=0, tiled=True)
    return lax.all_gather(own, axis, axis=0, tiled=True)[: len(lines)].reshape(value.shape)


def per_device(diag_block, panel, trailing):
    width = diag_block.shape[1]
    n_rows = lax.axis_size(PROW)
    n_cols = lax.axis_size(PCOL)
    prow_index = lax.axis_index(PROW)
    pcol_index = lax.axis_index(PCOL)
    whole_diag = gather_axes(diag_block, PROW_PCOL, (0, 2, 3, 1), 0)
    lower = jnp.linalg.cholesky(whole_diag)
    own_rows = diag_block.shape[0]
    factor_diag = lax.dynamic_slice_in_dim(
        lower, (prow_index * n_cols + pcol_index) * own_rows, own_rows, 0
    )
    rows = panel.reshape(-1, width)
    solved = jax.scipy.linalg.solve_triangular(lower, rows.T, lower=True).T
    factor_panel = solved.reshape(panel.shape)
    row_blocks = lax.all_gather(factor_panel, PCOL, axis=1, tiled=True)
    local_rows = row_blocks.shape[0]
    local_cols = trailing.shape[2]
    ratio = n_cols // n_rows
    root = pcol_index % n_rows
    offset = pcol_index // n_rows
    grouped = row_blocks.reshape(local_cols, ratio, width, width)
    chosen = lax.dynamic_index_in_dim(grouped, offset, 1, keepdims=False)
    col_blocks = spread(chosen, PROW, root)
    block_row = jnp.arange(local_rows, dtype=jnp.int32) * n_rows + prow_index
    block_col = jnp.arange(local_cols, dtype=jnp.int32) * n_cols + pcol_index
    pattern = (block_col[None, :] <= block_row[:, None]).astype(jnp.int32)
    weights = pattern.astype(jnp.float32)
    product = jnp.einsum("uik,vjk->uivj", row_blocks, col_blocks, precision=lax.Precision.HIGHEST)
    updated = trailing - weights[:, None, :, None] * product
    return (factor_diag, factor_panel, updated)


def solution(mesh):
    finer = Mesh(mesh.devices.reshape(4, 2, 4, 4), ("prow_0", "prow_1", "pcol_0", "pcol_1"))
    return jax.shard_map(
        per_device,
        mesh=finer,
        in_specs=(P(PROW_PCOL, None), P(None, PROW_PCOL, None), P(None, PROW, None, PCOL)),
        out_specs=(P(PROW_PCOL, None), P(None, PROW_PCOL, None), P(None, PROW, None, PCOL)),
        check_vma=False,
    )
```

profile of v0, /device:TPU:9, one launch (start us, length us, event | category | flops | bytes accessed | tf_op | source)
XLA Modules:
  0.0 354.7 jit_solution(13905995756323982596)
XLA Ops:
  7.2 9.5 %all-gather.4 = f32[4,4,512]{2,1,0:T(4,128)S(1)} all-gather(f32[1,4,512]{2,1,0:T(4,128)} %bitcast.85), channel_id=2, replica_groups=mesh['prow_0'=4,'prow_1'=2,'pcol_0'=4,'pcol_1'=4] {'prow_0'}, dimensions={0}, use_global_device_ids=true | all-gather | bytes 40960 | tf_op jit(solution)/shard_map/all_gather | solution.py:21
  16.7 9.4 %all-gather.1 = f32[16,4,512]{2,1,0:T(4,128)S(1)} all-gather(f32[4,4,512]{2,1,0:T(4,128)S(1)} %all-gather.4), channel_id=3, replica_groups=mesh['prow_0'=4,'prow_1'=2,'pcol_0'=4,'pcol_1'=4] {'pcol_0'}, dimensions={0}, use_global_device_ids=true | all-gather | bytes 163840 | tf_op jit(solution)/shard_map/all_gather | solution.py:21
  26.1 12.0 %all-gather.2 = f32[16,4,4,512]{3,2,1,0:T(4,128)} all-gather(f32[4,4,4,512]{3,2,1,0:T(4,128)S(1)} %bitcast.83), channel_id=4, replica_groups=mesh['prow_0'=4,'prow_1'=2,'pcol_0'=4,'pcol_1'=4] {'pcol_1'}, dimensions={0}, use_global_device_ids=true | all-gather | bytes 655360 | tf_op jit(solution)/shard_map/all_gather | solution.py:21
  39.3 19.8 %all-gather.13.cloned.1.call-done = f32[8,4,4,4,512]{4,3,2,1,0:T(4,128)} async-done(((f32[4,4,4,4,512]{4,3,2,1,0:T(4,128)}), f32[8,4,4,4,512]{4,3,2,1,0:T(4,128)}) %all-gather.13.cloned.1.call-update) | async-done | bytes 1048592 | tf_op jit(solution)/shard_map/all_gather | solution.py:21
  59.1 1.4 copy.22
  61.4 11.7 %cholesky.104 = f32[128,128]{1,0:T(8,128)S(1)} custom-call(f32[128,128]{1,0:T(8,128)S(1)} %cholesky.266), custom_call_target="Cholesky" | custom-call | tf_op jit(solution)/shard_map/jit(cholesky)/cholesky | solution.py:55
  73.2 9.8 %custom-call.31 = f32[1,128,128]{1,2,0:T(8,128)S(1)} custom-call(f32[1,128,128]{2,1,0:T(8,128)S(1)} %get-tuple-element.44), custom_call_target="InvertDiagBlocksLowerTriangular" | custom-call | tf_op jit(solution)/shard_map/jit(cholesky)/cholesky | solution.py:55
  83.8 11.7 %cholesky.217 = f32[128,128]{1,0:T(8,128)S(1)} custom-call(f32[128,128]{1,0:T(8,128)S(1)} %cholesky.270), custom_call_target="Cholesky" | custom-call | tf_op jit(solution)/shard_map/jit(cholesky)/cholesky | solution.py:55
  95.5 9.9 %custom-call.32 = f32[1,128,128]{1,2,0:T(8,128)S(1)} custom-call(f32[1,128,128]{2,1,0:T(8,128)S(1)} %get-tuple-element.41), custom_call_target="InvertDiagBlocksLowerTriangular" | custom-call | tf_op jit(solution)/shard_map/jit(cholesky)/cholesky | solution.py:55
  106.2 11.7 %cholesky.238 = f32[128,128]{1,0:T(8,128)S(1)} custom-call(f32[128,128]{1,0:T(8,128)S(1)} %cholesky.275), custom_call_target="Cholesky" | custom-call | tf_op jit(solution)/shard_map/jit(cholesky)/cholesky | solution.py:55
  118.6 9.8 %custom-call.33 = f32[1,128,128]{1,2,0:T(8,128)S(1)} custom-call(f32[1,128,128]{2,1,0:T(8,128)S(1)} %get-tuple-element.38), custom_call_target="InvertDiagBlocksLowerTriangular" | custom-call | tf_op jit(solution)/shard_map/jit(cholesky)/cholesky | solution.py:55
  129.1 11.9 %cholesky.255 = f32[128,128]{1,0:T(8,128)S(1)} custom-call(f32[128,128]{1,0:T(8,128)S(1)} %convolution_subtract_fusion.5), custom_call_target="Cholesky" | custom-call | tf_op jit(solution)/shard_map/jit(cholesky)/cholesky | solution.py:55
  145.0 10.5 %while.1 = (s32[]{:T(128)}, f32[512,512]{1,0:T(8,128)S(1)}, s32[4,2]{0,1:T(2,128)S(1)}, f32[4,128,128]{2,1,0:T(8,128)}, s32[]{:T(128)}) while((s32[]{:T(128)}, f32[512,512]{1,0:T(8,128)S(1)}, s32[4,2]{0,1:T(2,128)S(1)}, f32[4,128,128]{2,1,0:T(8,128)}, s32[]{:T(128)}) %tuple.36), condition=%wide.while_cond, body=%wide.while_body.sunk | while | flops 2 | bytes 132205 | solution.py:61
  145.6 2.0 bitcast_dynamic-update-slice_fusion.2
  148.3 2.0 bitcast_dynamic-update-slice_fusion.2
  150.9 2.0 bitcast_dynamic-update-slice_fusion.2
  153.5 2.0 bitcast_dynamic-update-slice_fusion.2
  155.5 40.1 %custom-call.34 = f32[4,128,128]{1,2,0:T(8,128)S(1)} custom-call(f32[4,128,128]{2,1,0:T(8,128)} %get-tuple-element.10), custom_call_target="InvertDiagBlocksLowerTriangular" | custom-call | tf_op jit(solution)/shard_map/jit(_solve_triangular)/triangular_solve | solution.py:61
  198.6 52.6 %all-gather.9.cloned.1.call-done = f32[4,512,512]{2,1,0:T(8,128)} async-done(((f32[4,32,512]{2,1,0:T(8,128)}), f32[4,512,512]{2,1,0:T(8,128)}) %all-gather.9.cloned.1.call-update) | async-done | bytes 4194320 | tf_op jit(solution)/shard_map/all_gather | solution.py:63
  251.1 3.1 dynamic-slice_select_fusion
  254.4 29.5 %reduce-scatter.2.cloned.1.call-done = f32[128,512]{1,0:T(8,128)} async-done(((f32[1024,512]{1,0:T(8,128)}), f32[128,512]{1,0:T(8,128)}) %reduce-scatter.2.cloned.1.call-update) | async-done | bytes 262160 | tf_op jit(solution)/shard_map/reduce_scatter | solution.py:44
  284.6 28.1 %all-gather.11.cloned.1.call-done = f32[1024,512]{1,0:T(8,128)} async-done(((f32[128,512]{1,0:T(8,128)}), f32[1024,512]{1,0:T(8,128)}) %all-gather.11.cloned.1.call-update) | async-done | bytes 2097168 | tf_op jit(solution)/shard_map/all_gather | solution.py:45
  312.7 18.5 %copy_subtract_fusion = f32[4,512,2,512]{3,1,2,0:T(8,128)S(1)} fusion(f32[4,512,2,512]{3,2,1,0:T(2,128)} %param.5, f32[4,2]{1,0:T(4,128)S(1)} %convert_convert_fusion, f32[2,512,512,1]{2,1,0,3:T(8,128)} %bitcast.75, f32[4,512,512]{2,1,0:T(8,128)} %all-gather.9.cloned.1.call-done), kind=kOutput, calls=%fused_computation.2 | convolution fusion | flops 12889096192 | bytes 23068704 | tf_op jit(solution)/shard_map/uik,vjk->uivj/dot_general | solution.py:76
  331.2 17.0 %copy.27 = f32[4,512,2,512]{3,2,1,0:T(2,128)} copy(f32[4,512,2,512]{3,1,2,0:T(8,128)S(1)} %copy_subtract_fusion) | data formatting | bytes 16777216
  (54 shorter events, 12.5 us)
Async XLA Ops:
  7.2 52.0 %all-gather.13.cloned.1.call-start = ((), (), s32[]{:S(2)}) async-start(), calls=%async_computation.4 | async-start | bytes 1572864 | tf_op jit(solution)/shard_map/all_gather | solution.py:21
  38.2 213.0 %all-gather.9.cloned.1.call-start = ((), (), s32[]{:S(2)}) async-start(), calls=%async_computation.1 | async-start | bytes 4456448 | tf_op jit(solution)/shard_map/all_gather | solution.py:63
  198.5 85.4 %reduce-scatter.2.cloned.1.call-start = ((), (), s32[]{:S(2)}) async-start(), calls=%async_computation.2 | async-start | bytes 2359296 | tf_op jit(solution)/shard_map/reduce_scatter | solution.py:44
  254.3 58.4 %all-gather.11.cloned.1.call-start = ((), (), s32[]{:S(2)}) async-start(), calls=%async_computation.3 | async-start | bytes 2359296 | tf_op jit(solution)/shard_map/all_gather | solution.py:45
Sparse Core Ops, SparseCore 0:
  38.3 20.7 all-gather.12
  198.6 52.4 all-gather.8
  254.4 29.4 reduce-scatter.1
  285.4 27.2 all-gather.10
where the time goes:
time: 357 us; the launch traced here: 355 us
  waiting for transfers between devices  130 us (36%)
  other arithmetic  123 us (34%)
  local copies, waits for them, and re-layouts  32.1 us (9%)
  blocking collectives  30.9 us (9%)
  matrix products  22.3 us (6%)
  between operations  16.6 us (5%)
    another operation x14, other arithmetic, per_device(): lower = jnp.linalg.cholesky(whole_diag)  78.7 us
    all_gather x1, waiting for transfers between devices, per_device(): row_blocks = lax.all_gather(factor_panel, PCOL, axis=1, tiled=True)  52.6 us
    another operation x3, other arithmetic, per_device(): solved = jax.scipy.linalg.solve_triangular(lower, rows.T, lower=True).T  40.4 us
    all_gather x3, blocking collectives, stacked_from(): blocks = lax.all_gather(blocks, axes[k])  30.9 us
    reduce_scatter x1, waiting for transfers between devices, spread(): own = lax.psum_scatter(padded, axis, scatter_dimension=0, tiled=True)  29.5 us
    all_gather x1, waiting for transfers between devices, spread(): lax.all_gather(own, axis, axis=0, tiled=True)[:len(lines)]  28.1 us
    all_gather x1, waiting for transfers between devices, stacked_from(): blocks = lax.all_gather(blocks, axes[k])  19.8 us
    dot_general x1, matrix products, per_device(): jnp.einsum('uik,vjk->uivj', row_blocks, col_blocks, precision=lax.Precisi...  18.5 us
  transfers between devices with their start and end apart: 4, of which 4 were waited for; matrix products, arithmetic and copies ran while one was open for 0% of the time, Pallas kernels for 0%

commit v1 on v0

v1 whole, which is shorter than its diff:
```python
import functools

import jax
import jax.numpy as jnp
from jax import lax
from jax.experimental import pallas as pl
from jax.experimental.pallas import tpu as pltpu
from jax.sharding import Mesh
from jax.sharding import PartitionSpec as P

PROW = ("prow_0", "prow_1")
PCOL = ("pcol_0", "pcol_1")
PROW_PCOL = ("prow_0", "prow_1", "pcol_0", "pcol_1")


def in_order(blocks, dim):
    blocks = jnp.moveaxis(blocks, 0, dim)
    dims = blocks.shape
    return blocks.reshape(*dims[:dim], dims[dim] * dims[dim + 1], *dims[dim + 2 :])


def stacked_from(value, axes, turns):
    blocks = value
    for k in turns:
        blocks = lax.all_gather(blocks, axes[k])
    done = turns[::-1]
    back = [done.index(k) for k in range(len(axes))]
    blocks = blocks.transpose(*back, *range(len(axes), blocks.ndim))
    return blocks.reshape(-1, *value.shape)


def gather_axes(value, axes, turns, dim):
    return in_order(stacked_from(value, axes, turns), dim)


def padded_to(lines, peers):
    spare = -lines.shape[0] % peers
    if not spare:
        return lines
    return jnp.concatenate([lines, jnp.zeros((spare, *lines.shape[1:]), lines.dtype)])


def spread(value, axis, root):
    lines = jnp.where(lax.axis_index(axis) == root, value, jnp.zeros_like(value)).reshape(
        -1, *value.shape[1:][-1:]
    )
    padded = padded_to(lines, lax.axis_size(axis))
    own = lax.psum_scatter(padded, axis, scatter_dimension=0, tiled=True)
    return lax.all_gather(own, axis, axis=0, tiled=True)[: len(lines)].reshape(value.shape)


HI = lax.Precision.HIGHEST
F32 = jnp.float32

def tdot(a, b, prec=HI):
    return lax.dot_general(a, b, (((0,), (0,)), ((), ())), precision=prec, preferred_element_type=F32)

def bc(col, n=128):
    return jnp.broadcast_to(col, (col.shape[0], n))

def elim8(G, c0, sub):
    n = len(G)
    C = [[bc(G[g][:, c0 + j:c0 + j + 1]) for j in range(8)] for g in range(n)]
    L = [G[g][:, :128] for g in range(n)]
    V = [G[g][:, 128:] for g in range(n)]
    dv = None
    for j in range(8):
        piv = [jnp.broadcast_to(C[0][l][j:j + 1, :], (8, 128)) for l in range(j, 8)]
        rinv = 1.0 / piv[0]
        rowL = jnp.broadcast_to(L[0][j:j + 1, :], (8, 128))
        rowV = jnp.broadcast_to(V[0][j:j + 1, :], (8, 128))
        dv = piv[0] if j == 0 else jnp.where(sub == j, piv[0], dv)
        for g in range(n):
            m = C[g][j] * rinv
            if g == 0:
                m = jnp.where(sub > j, m, 0.0)
            for l in range(j + 1, 8):
                C[g][l] = C[g][l] - m * piv[l - j]
            L[g] = L[g] - m * rowL
            V[g] = V[g] - m * rowV
    sc = lax.rsqrt(dv)
    L[0] = L[0] * sc
    V[0] = V[0] * sc
    return [jnp.concatenate([L[g], V[g]], 1) for g in range(n)]

def leaf(T):
    sub = lax.broadcasted_iota(jnp.int32, (8, 128), 0)
    for sb in range(4):
        r0 = 32 * sb
        G = [T[r0 + 8 * g:r0 + 8 * g + 8, :] for g in range(4)]
        done = []
        for g in range(4):
            G = elim8(G, r0 + 8 * g, sub)
            done.append(G[0])
            T[r0 + 8 * g:r0 + 8 * g + 8, :] = G[0]
            G = G[1:]
        if sb < 3:
            W = jnp.concatenate(done, 0)
            Pm = tdot(W[:, :128], W)
            T[r0 + 32:128, :] = T[r0 + 32:128, :] - Pm[r0 + 32:128, :]

def chol_body(M, T, U, nb=4):
    row = lax.broadcasted_iota(jnp.int32, (128, 128), 0)
    col = lax.broadcasted_iota(jnp.int32, (128, 128), 1)
    eye = jnp.where(row == col, 1.0, 0.0).astype(F32)
    n = nb * 128
    for k in range(nb):
        a, b = k * 128, (k + 1) * 128
        T[:, :128] = M[a:b, a:b]
        T[:, 128:] = eye
        leaf(T)
        Ukk = jnp.where(col >= row, T[:, :128], 0.0)
        Vkk = jnp.where(col <= row, T[:, 128:], 0.0)
        U[a:b, a:b] = Ukk
        if k > 0:
            U[a:b, :a] = jnp.zeros((128, a), F32)
            M[a:b, :a] = jnp.dot(Vkk, M[a:b, :a], precision=HI, preferred_element_type=F32)
        M[a:b, a:b] = Vkk
        if k < nb - 1:
            Ur = jnp.dot(Vkk, M[a:b, b:], precision=HI, preferred_element_type=F32)
            U[a:b, b:] = Ur
            M[a:b, b:] = jnp.zeros((128, n - b), F32)
            if k > 0:
                M[b:, :a] = M[b:, :a] - tdot(Ur, M[a:b, :a])
            M[b:, a:b] = -tdot(Ur, Vkk)
            M[b:, b:] = M[b:, b:] - tdot(Ur, Ur)
F32 = jnp.float32
BF16 = jnp.bfloat16

def halves(x):
    hi = x.astype(BF16)
    return hi, (x - hi.astype(F32)).astype(BF16)

def left3(x):
    hi, lo = halves(x)
    return jnp.concatenate([hi, hi, lo], 1)

def right3(x):
    hi, lo = halves(x)
    return jnp.concatenate([hi, lo, hi], 1)

def ndot(a, b):
    return lax.dot_general(a, b, (((1,), (1,)), ((), ())), preferred_element_type=F32)

def solve_rows(x, l0, l1):
    return jnp.concatenate([ndot(left3(x[:, :256]), l0), ndot(left3(x), l1)], 1)

def update_kernel(p_of, q_of, inv, xcol, xrow, c, fpan, out, l0, l1, cols, fs):
    step = pl.program_id(0)
    p, q = p_of(), q_of()
    u, h = step // 2, step % 2

    @pl.when(step == 0)
    def _():
        l0[...] = right3(inv[:256, :256])
        l1[...] = right3(inv[256:, :])
        for k in range(4):
            cols[256 * k:256 * (k + 1), :] = right3(solve_rows(xcol[256 * k:256 * (k + 1), :], l0[...], l1[...]))

    f = solve_rows(xrow[...], l0[...], l1[...])
    fs[...] = f

    @pl.when(q // 8 == h)
    def _():
        fpan[0] = fs[pl.ds(pl.multiple_of((q % 8) * 32, 32), 32), :]

    f3 = left3(f)
    for v in range(2):
        present = v * 16 + q <= u * 8 + p

        @pl.when(present)
        def _():
            prod = ndot(f3, cols[512 * v:512 * (v + 1), :])
            for t in range(4):
                at = pl.ds(2 * t + v, 256, stride=8)
                out[at, :] = c[at, :] - prod[:, 128 * t:128 * (t + 1)]

        @pl.when(jnp.logical_not(present))
        def _():
            for t in range(4):
                at = pl.ds(2 * t + v, 256, stride=8)
                out[at, :] = c[at, :]

def update(p_of, q_of, inv, xcol, xrow, c):
    whole = lambda s: (0, 0)
    return pl.pallas_call(
        functools.partial(update_kernel, p_of, q_of),
        grid=(8,),
        in_specs=[
            pl.BlockSpec((512, 512), whole),
            pl.BlockSpec((1024, 512), whole),
            pl.BlockSpec((256, 512), lambda s: (s, 0)),
            pl.BlockSpec((2048, 128), lambda s: (s, 0)),
        ],
        out_specs=[
            pl.BlockSpec((1, 32, 512), lambda s: (s // 2, 0, 0)),
            pl.BlockSpec((2048, 128), lambda s: (s, 0)),
        ],
        out_shape=[jax.ShapeDtypeStruct((4, 32, 512), F32), jax.ShapeDtypeStruct((16384, 128), F32)],
        scratch_shapes=[pltpu.VMEM((256, 768), BF16), pltpu.VMEM((256, 1536), BF16),
                        pltpu.VMEM((1024, 1536), BF16), pltpu.VMEM((256, 512), F32)],
        compiler_params=pltpu.CompilerParams(vmem_limit_bytes=50 << 20),
        name="panel_update",
    )(inv, xcol, xrow, c)


def factor_kernel(a_ref, inv_ref, upper_ref, M, T):
    M[...] = a_ref[...]
    chol_body(M, T, upper_ref)
    inv_ref[...] = M[...]


def factor(a):
    return pl.pallas_call(
        factor_kernel,
        out_shape=[jax.ShapeDtypeStruct((512, 512), F32)] * 2,
        scratch_shapes=[pltpu.VMEM((512, 512), F32), pltpu.VMEM((128, 256), F32)],
        name="factor",
        cost_estimate=pl.CostEstimate(flops=10**10, bytes_accessed=3 << 20, transcendentals=0),
    )(a)


def per_device(diag_block, panel, trailing):
    p, q = lax.axis_index(PROW), lax.axis_index(PCOL)
    whole_diag = gather_axes(diag_block, PROW_PCOL, (0, 2, 3, 1), 0)
    row_blocks = lax.all_gather(panel, PCOL, axis=1, tiled=True)
    grouped = row_blocks.reshape(2, 2, 512, 512)
    chosen = lax.dynamic_index_in_dim(grouped, q // 8, 1, keepdims=False)
    col_blocks = spread(chosen, PROW, q % 8)
    inv, upper = factor(whole_diag)
    factor_diag = lax.dynamic_slice(upper, (0, (p * 16 + q) * 4), (512, 4)).T
    c = trailing.reshape(4, 512, 2, 4, 128).transpose(0, 1, 3, 2, 4).reshape(16384, 128)
    factor_panel, out = update(
        lambda: lax.axis_index(PROW), lambda: lax.axis_index(PCOL),
        inv, col_blocks.reshape(1024, 512), row_blocks.reshape(2048, 512), c,
    )
    updated = out.reshape(4, 512, 4, 2, 128).transpose(0, 1, 3, 2, 4).reshape(4, 512, 2, 512)
    return factor_diag, factor_panel, updated


def solution(mesh):
    finer = Mesh(mesh.devices.reshape(4, 2, 4, 4), ("prow_0", "prow_1", "pcol_0", "pcol_1"))
    specs = (P(PROW_PCOL, None), P(None, PROW_PCOL, None), P(None, PROW, None, PCOL))
    return jax.shard_map(per_device, mesh=finer, in_specs=specs, out_specs=specs, check_vma=False)
```

time: 357 us -> 176 us (0.49)
  other arithmetic: 123 us -> 3.13 us
  waiting for transfers between devices: 130 us -> 76.2 us
  Pallas kernels: 0 us -> 40.9 us
  local copies, waits for them, and re-layouts: 32.1 us -> 7.92 us
  matrix products: 22.3 us -> 0 us
    another operation x17 -> x0, other arithmetic: 119 us -> none  [the longest x14 78.7 us: per_device(): lower = jnp.linalg.cholesky(whole_diag)]
    pallas_call x0 -> x2, Pallas kernels: none -> 40.9 us  [the longest x1 22.6 us: factor(): pl.pallas_call(factor_kernel, out_shape=[jax.ShapeDtypeStruct((512, 512),...]
    reduce_scatter x1, waiting for transfers between devices: 29.5 us -> 0.02 us  [spread(): own = lax.psum_scatter(padded, axis, scatter_dimension=0, tiled=True)]
    all_gather x1, waiting for transfers between devices: 28.1 us -> 0.01 us  [spread(): lax.all_gather(own, axis, axis=0, tiled=True)[:len(lines)]]
    dot_general x1 -> x0, matrix products: 18.5 us -> none  [per_device(): jnp.einsum('uik,vjk->uivj', row_blocks, col_blocks, precision=lax.Precisi...]
    unnamed x1 -> x7, local copies, waits for them, and re-layouts: 17 us -> 4.15 us
    another operation x17 -> x0, local copies, waits for them, and re-layouts: 10.6 us -> none
    another operation x13 -> x0, matrix products: 3.8 us -> none  [the longest x7 1.92 us: per_device(): solved = jax.scipy.linalg.solve_triangular(lower, rows.T, lower=True).T]
  transfers between devices with their start and end apart: 4 -> 4, of which waited for: 4 -> 2; matrix products, arithmetic and copies ran while one was open for 0% -> 3% of each run, Pallas kernels for 0% -> 13%
where the time goes in v1:
time: 176 us; the launch traced here: 173 us
  waiting for transfers between devices  76.2 us (43%)
  Pallas kernels  40.9 us (23%)
  blocking collectives  29.4 us (17%)
  between operations  15.6 us (9%)
  local copies, waits for them, and re-layouts  7.92 us (4%)
  other arithmetic  3.13 us (2%)
    all_gather x1, waiting for transfers between devices, per_device(): row_blocks = lax.all_gather(panel, PCOL, axis=1, tiled=True)  56.2 us
    all_gather x3, blocking collectives, stacked_from(): blocks = lax.all_gather(blocks, axes[k])  29.4 us
    pallas_call x1, Pallas kernels, factor(): pl.pallas_call(factor_kernel, out_shape=[jax.ShapeDtypeStruct((512, 512),...  22.6 us
    all_gather x1, waiting for transfers between devices, stacked_from(): blocks = lax.all_gather(blocks, axes[k])  18.7 us
    pallas_call x1, Pallas kernels, update(): pl.pallas_call(functools.partial(update_kernel, p_of, q_of), grid=(8,), i...  18.3 us
    unnamed x7, local copies, waits for them, and re-layouts  4.15 us
  transfers between devices with their start and end apart: 4, of which 2 were waited for; matrix products, arithmetic and copies ran while one was open for 3% of the time, Pallas kernels for 13%

profile of v1, /device:TPU:9, one launch (start us, length us, event | category | flops | bytes accessed | tf_op | source)
XLA Modules:
  0.0 173.2 jit_solution(17059469875696428422)
XLA Ops:
  8.0 0.0 all-gather.9.cloned.1.call-start
  8.0 0.7 all-gather.9.cloned.1.call-update
  8.7 0.0 reduce-scatter.2.cloned.1.call-start
  8.8 56.2 %all-gather.9.cloned.1.call-done = f32[4,512,512]{2,1,0:T(8,128)} async-done(((f32[4,32,512]{2,1,0:T(8,128)}), f32[4,512,512]{2,1,0:T(8,128)}) %all-gather.9.cloned.1.call-update) | async-done | bytes 4194320 | tf_op jit(solution)/shard_map/all_gather | solution.py:226
  65.1 3.1 %bitcast_select_fusion = f32[2,1,512,512]{3,2,0,1:T(8,128)} fusion(f32[2,2,512,512]{3,2,1,0:T(8,128)} %bitcast.23, s32[]{:T(128)S(6)} %select_n.34, pred[]{:T(512)S(6)} %eq.5), kind=kLoop, calls=%fused_computation | loop fusion | flops 524288 | bytes 4194309 | tf_op jit(solution)/shard_map/jit(_where)/select_n | solution.py:44
  68.2 0.0 reduce-scatter.2.cloned.1.call-update
  68.2 0.0 all-gather.13.cloned.1.call-start
  68.3 0.6 copy-done.2
  68.9 9.4 %all-gather.4 = f32[4,4,512]{2,1,0:T(4,128)S(1)} all-gather(f32[1,4,512]{2,1,0:T(4,128)S(1)} %bitcast.30), channel_id=2, replica_groups=mesh['prow_0'=4,'prow_1'=2,'pcol_0'=4,'pcol_1'=4] {'prow_0'}, dimensions={0}, use_global_device_ids=true | all-gather | bytes 40960 | tf_op jit(solution)/shard_map/all_gather | solution.py:25
  78.3 9.4 %all-gather.1 = f32[16,4,512]{2,1,0:T(4,128)S(1)} all-gather(f32[4,4,512]{2,1,0:T(4,128)S(1)} %all-gather.4), channel_id=3, replica_groups=mesh['prow_0'=4,'prow_1'=2,'pcol_0'=4,'pcol_1'=4] {'pcol_0'}, dimensions={0}, use_global_device_ids=true | all-gather | bytes 163840 | tf_op jit(solution)/shard_map/all_gather | solution.py:25
  87.7 10.6 %all-gather.2 = f32[16,4,4,512]{3,2,1,0:T(4,128)} all-gather(f32[4,4,4,512]{3,2,1,0:T(4,128)S(1)} %bitcast.29), channel_id=4, replica_groups=mesh['prow_0'=4,'prow_1'=2,'pcol_0'=4,'pcol_1'=4] {'pcol_1'}, dimensions={0}, use_global_device_ids=true | all-gather | bytes 655360 | tf_op jit(solution)/shard_map/all_gather | solution.py:25
  98.3 0.0 all-gather.13.cloned.1.call-update
  98.3 0.0 all-gather.11.cloned.1.call-start
  98.4 0.0 reduce-scatter.2.cloned.1.call-done
  98.4 0.5 all-gather.11.cloned.1.call-update
  98.9 18.7 %all-gather.13.cloned.1.call-done = f32[8,4,4,4,512]{4,3,2,1,0:T(4,128)} async-done(((f32[4,4,4,4,512]{4,3,2,1,0:T(4,128)}), f32[8,4,4,4,512]{4,3,2,1,0:T(4,128)}) %all-gather.13.cloned.1.call-update) | async-done | bytes 1048592 | tf_op jit(solution)/shard_map/all_gather | solution.py:25
  117.6 1.4 copy.15
  119.0 1.3 reshape_reshape.3.a_ref
  120.3 22.6 %factor.1 = (f32[512,512]{1,0:T(8,128)}, f32[512,512]{1,0:T(8,128)}) custom-call(f32[512,512]{1,0:T(8,128)} %reshape_reshape.3.a_ref), custom_call_target="tpu_custom_call" | custom-call | flops 10000000000 | bytes 3145728 | tf_op jit(solution)/shard_map/factor/pallas_call | solution.py:214
  142.9 1.1 dynamic-slice_bitcast_fusion
  144.0 0.7 copy.19
  144.7 1.6 copy-done
  146.3 1.2 copy-done.1
  147.5 18.3 %panel_update.1 = (f32[4,32,512]{2,1,0:T(8,128)}, f32[16384,128]{1,0:T(8,128)}) custom-call(f32[512,512]{1,0:T(8,128)S(1)} %copy-done.1, f32[1024,512]{1,0:T(8,128)S(1)} %copy-done, f32[2048,512]{1,0:T(8,128)} %bitcast.24, f32[16384,128]{1,0:T(8,128)} %bitcast.26), custom_call_target="tpu_custom_call" | custom-call | tf_op jit(solution)/shard_map/panel_update/pallas_call | solution.py:186
  (4 shorter events, 0.0 us)
Async XLA Ops:
  8.0 57.1 %all-gather.9.cloned.1.call-start = ((), (), s32[]{:S(2)}) async-start(), calls=%async_computation.1 | async-start | bytes 4456448 | tf_op jit(solution)/shard_map/all_gather | solution.py:226
  8.7 89.7 %reduce-scatter.2.cloned.1.call-start = ((), (), s32[]{:S(2)}) async-start(), calls=%async_computation.2 | async-start | bytes 2359296 | tf_op jit(solution)/shard_map/reduce_scatter | solution.py:48
  68.2 0.7 copy-start.2
  68.2 49.4 %all-gather.13.cloned.1.call-start = ((), (), s32[]{:S(2)}) async-start(), calls=%async_computation.4 | async-start | bytes 1572864 | tf_op jit(solution)/shard_map/all_gather | solution.py:25
  98.3 46.4 %all-gather.11.cloned.1.call-start = ((), (), s32[]{:S(2)}) async-start(), calls=%async_computation.3 | async-start | bytes 2359296 | tf_op jit(solution)/shard_map/all_gather | solution.py:49
  144.7 1.6 copy-start
  146.3 1.2 copy-start.1
Sparse Core Ops, SparseCore 0:
  11.0 53.9 all-gather.8
  68.3 29.4 reduce-scatter.1
Sparse Core Ops, SparseCore 1:
  98.4 19.1 all-gather.12
  119.2 25.3 all-gather.10

commit v2 on v1

v2 whole, which is shorter than its diff:
```python
import functools

import jax
import jax.numpy as jnp
from jax import lax
from jax.experimental import pallas as pl
from jax.experimental.pallas import tpu as pltpu
from jax.sharding import PartitionSpec as P

F32 = jnp.float32
BF16 = jnp.bfloat16
HI = lax.Precision.HIGHEST
MESH = pl.DeviceIdType.MESH


def tdot(a, b, prec=HI):
    return lax.dot_general(a, b, (((0,), (0,)), ((), ())), precision=prec, preferred_element_type=F32)

def bc(col, n=128):
    return jnp.broadcast_to(col, (col.shape[0], n))

def elim8(G, c0, sub):
    n = len(G)
    C = [[bc(G[g][:, c0 + j:c0 + j + 1]) for j in range(8)] for g in range(n)]
    L = [G[g][:, :128] for g in range(n)]
    V = [G[g][:, 128:] for g in range(n)]
    dv = None
    for j in range(8):
        piv = [jnp.broadcast_to(C[0][l][j:j + 1, :], (8, 128)) for l in range(j, 8)]
        rinv = 1.0 / piv[0]
        rowL = jnp.broadcast_to(L[0][j:j + 1, :], (8, 128))
        rowV = jnp.broadcast_to(V[0][j:j + 1, :], (8, 128))
        dv = piv[0] if j == 0 else jnp.where(sub == j, piv[0], dv)
        for g in range(n):
            m = C[g][j] * rinv
            if g == 0:
                m = jnp.where(sub > j, m, 0.0)
            for l in range(j + 1, 8):
                C[g][l] = C[g][l] - m * piv[l - j]
            L[g] = L[g] - m * rowL
            V[g] = V[g] - m * rowV
    sc = lax.rsqrt(dv)
    L[0] = L[0] * sc
    V[0] = V[0] * sc
    return [jnp.concatenate([L[g], V[g]], 1) for g in range(n)]

def leaf(T, hook, k):
    sub = lax.broadcasted_iota(jnp.int32, (8, 128), 0)
    for sb in range(4):
        r0 = 32 * sb
        G = [T[r0 + 8 * g:r0 + 8 * g + 8, :] for g in range(4)]
        done = []
        for g in range(4):
            G = elim8(G, r0 + 8 * g, sub)
            done.append(G[0])
            T[r0 + 8 * g:r0 + 8 * g + 8, :] = G[0]
            G = G[1:]
        hook(4 * k + sb)
        if sb < 3:
            W = jnp.concatenate(done, 0)
            Pm = tdot(W[:, :128], W)
            T[r0 + 32:128, :] = T[r0 + 32:128, :] - Pm[r0 + 32:128, :]

def chol_body(M, T, U, hook, nb=4):
    row = lax.broadcasted_iota(jnp.int32, (128, 128), 0)
    col = lax.broadcasted_iota(jnp.int32, (128, 128), 1)
    eye = jnp.where(row == col, 1.0, 0.0).astype(F32)
    n = nb * 128
    for k in range(nb):
        a, b = k * 128, (k + 1) * 128
        T[:, :128] = M[a:b, a:b]
        T[:, 128:] = eye
        leaf(T, hook, k)
        Ukk = jnp.where(col >= row, T[:, :128], 0.0)
        Vkk = jnp.where(col <= row, T[:, 128:], 0.0)
        U[a:b, a:b] = Ukk
        if k > 0:
            U[a:b, :a] = jnp.zeros((128, a), F32)
            M[a:b, :a] = jnp.dot(Vkk, M[a:b, :a], precision=HI, preferred_element_type=F32)
        M[a:b, a:b] = Vkk
        if k < nb - 1:
            Ur = jnp.dot(Vkk, M[a:b, b:], precision=HI, preferred_element_type=F32)
            U[a:b, b:] = Ur
            M[a:b, b:] = jnp.zeros((128, n - b), F32)
            if k > 0:
                M[b:, :a] = M[b:, :a] - tdot(Ur, M[a:b, :a])
            M[b:, a:b] = -tdot(Ur, Vkk)
            M[b:, b:] = M[b:, b:] - tdot(Ur, Ur)


def halves(x):
    hi = x.astype(BF16)
    return hi, (x - hi.astype(F32)).astype(BF16)


def left3(x):
    hi, lo = halves(x)
    return jnp.concatenate([hi, hi, lo], 1)


def right3(x):
    hi, lo = halves(x)
    return jnp.concatenate([hi, lo, hi], 1)


def ndot(a, b):
    return lax.dot_general(a, b, (((1,), (1,)), ((), ())), preferred_element_type=F32)


def solve_rows(x, l0, l1):
    return jnp.concatenate([ndot(left3(x[:, :256]), l0), ndot(left3(x), l1)], 1)


def update_kernel(inv, lblk, xcol, xrow, c, fdiag, fpan, out, l0, l1, cols, fs):
    step = pl.program_id(0)
    p, q = lax.axis_index("prow"), lax.axis_index("pcol")
    u, h = step // 2, step % 2

    @pl.when(step == 0)
    def _():
        pair = lblk[pl.ds(pl.multiple_of((p % 2) * 64 + (q // 2) * 8, 8), 8), :]
        fdiag[...] = jnp.where(q % 2 == 0, pair[:4], pair[4:])
        l0[...] = right3(inv[:256, :256])
        l1[...] = right3(inv[256:, :])
        for k in range(4):
            cols[256 * k:256 * (k + 1), :] = right3(solve_rows(xcol[256 * k:256 * (k + 1), :], l0[...], l1[...]))

    f = solve_rows(xrow[...], l0[...], l1[...])
    fs[...] = f

    @pl.when(q // 8 == h)
    def _():
        fpan[0] = fs[pl.ds(pl.multiple_of((q % 8) * 32, 32), 32), :]

    f3 = left3(f)
    for v in range(2):
        present = v * 16 + q <= u * 8 + p

        @pl.when(present)
        def _():
            prod = ndot(f3, cols[512 * v:512 * (v + 1), :])
            for t in range(4):
                at = pl.ds(2 * t + v, 256, stride=8)
                out[at, :] = c[at, :] - prod[:, 128 * t:128 * (t + 1)]

        @pl.when(jnp.logical_not(present))
        def _():
            for t in range(4):
                at = pl.ds(2 * t + v, 256, stride=8)
                out[at, :] = c[at, :]


def update(inv, lblk, xcol, xrow, c):
    whole = lambda s: (0, 0)
    return pl.pallas_call(
        update_kernel,
        grid=(8,),
        in_specs=[
            pl.BlockSpec((512, 512), whole),
            pl.BlockSpec((128, 512), whole),
            pl.BlockSpec((1024, 512), whole),
            pl.BlockSpec((256, 512), lambda s: (s, 0)),
            pl.BlockSpec((2048, 128), lambda s: (s, 0)),
        ],
        out_specs=[
            pl.BlockSpec((4, 512), whole),
            pl.BlockSpec((1, 32, 512), lambda s: (s // 2, 0, 0)),
            pl.BlockSpec((2048, 128), lambda s: (s, 0)),
        ],
        out_shape=[jax.ShapeDtypeStruct((4, 512), F32), jax.ShapeDtypeStruct((4, 32, 512), F32),
                   jax.ShapeDtypeStruct((16384, 128), F32)],
        scratch_shapes=[pltpu.VMEM((256, 768), BF16), pltpu.VMEM((256, 1536), BF16),
                        pltpu.VMEM((1024, 1536), BF16), pltpu.VMEM((256, 512), F32)],
        compiler_params=pltpu.CompilerParams(vmem_limit_bytes=50 << 20),
        name="panel_update",
    )(inv, lblk, xcol, xrow, c)


def gather_factor_kernel(hooks, d, panel, inv, lblk, xrow, xcol, D, M, T, U, s1s, s1r, s2s, s2r, s3s, s3r, rs, rr, cs, cr, loc):
    p, q = lax.axis_index("prow"), lax.axis_index("pcol")
    y, c, x, z = p // 2, p % 2, q // 4, q % 4

    def at(dx, dy, dz, dc=0):
        return (lax.rem(y + dy, 4) * 2 + lax.rem(c + dc, 2), lax.rem(x + dx, 4) * 4 + lax.rem(z + dz, 4))

    def send(src, dst, ssem, rsem, dev):
        return pltpu.make_async_remote_copy(src_ref=src, dst_ref=dst, send_sem=ssem, recv_sem=rsem, device_id=dev, device_id_type=MESH)

    plane = [(dx, dz) for dx in range(4) for dz in range(4) if dx or dz]
    barrier = pltpu.get_barrier_semaphore()
    for dev in [at(dx, 0, dz) for dx, dz in plane] + [at(0, dy, 0) for dy in (1, 2, 3)] + [at(0, 0, 0, 1)]:
        pl.semaphore_signal(barrier, inc=1, device_id=dev, device_id_type=MESH)
    pl.semaphore_wait(barrier, 19)

    a0 = [send(d.at[0], D.at[y, c, q, 0], s1s.at[k], s1r.at[k], at(dx, 0, dz)) for k, (dx, dz) in enumerate(plane)]
    a1 = [send(d.at[1], D.at[y, c, q, 1], s1s.at[14 + dy], s1r.at[14 + dy], at(0, dy, 0)) for dy in (1, 2, 3)]
    for cp in a1 + a0:
        cp.start()
    D[y, c, q] = d[...]
    own = pltpu.make_async_copy(panel, xrow.at[:, x, z], loc.at[0])
    own.start()
    for cp in a1:
        cp.wait_recv()
    b1 = [send(D.at[:, c, q, 1], D.at[:, c, q, 1], s2s.at[k], s2r.at[k], at(dx, 0, dz)) for k, (dx, dz) in enumerate(plane)]
    for cp in b1:
        cp.start()
    for cp in a0:
        cp.wait_recv()
    b0 = [send(D.at[y, c, :, 0], D.at[y, c, :, 0], s2s.at[14 + dy], s2r.at[14 + dy], at(0, dy, 0)) for dy in (1, 2, 3)]
    for cp in b0:
        cp.start()
    for cp in b1:
        cp.wait_recv()
    c1 = send(D.at[:, c, :, 1], D.at[:, c, :, 1], s3s.at[1], s3r.at[1], at(0, 0, 0, 1))
    c1.start()
    for cp in b0:
        cp.wait_recv()
    c0 = send(D.at[:, c, :, 0], D.at[:, c, :, 0], s3s.at[0], s3r.at[0], at(0, 0, 0, 1))
    c0.start()

    def line(ref, u, first_z, off):
        if first_z:
            return ref.at[u, lax.rem(x + off, 4)]
        return ref.at[u, :, lax.rem(z + off, 4)]

    def shard(u, off):
        if u < 2:
            return xrow.at[u, x, lax.rem(z + off, 4)]
        return xrow.at[u, lax.rem(x + off, 4), z]

    def near(u, n):
        return at(0, 0, n) if u < 2 else at(n, 0, 0)

    def far(u, n):
        return at(n, 0, 0) if u < 2 else at(0, 0, n)

    row = {}
    for u in range(4):
        fwd, back = (1, 3) if u % 2 == 0 else (3, 1)
        mine = panel.at[u]
        spot = xrow.at[u, x, z]
        row[u] = [
            [send(mine, spot, rs.at[u, 0], rr.at[u, 0], near(u, 1)), send(mine, spot, rs.at[u, 1], rr.at[u, 1], near(u, 3))],
            [send(shard(u, back), shard(u, back), rs.at[u, 2], rr.at[u, 2], near(u, fwd))],
            [send(line(xrow, u, u < 2, 0), line(xrow, u, u < 2, 0), rs.at[u, 3], rr.at[u, 3], far(u, 1)),
             send(line(xrow, u, u < 2, 0), line(xrow, u, u < 2, 0), rs.at[u, 4], rr.at[u, 4], far(u, 3))],
            [send(line(xrow, u, u < 2, back), line(xrow, u, u < 2, back), rs.at[u, 5], rr.at[u, 5], far(u, fwd))],
        ]

    def row_start(u, s):
        for cp in row[u][s]:
            cp.start()

    def row_wait(u, s):
        for cp in row[u][s]:
            cp.wait_recv()

    root_p = lax.rem(q, 8)
    same = c == root_p % 2
    lag = lax.rem(y - root_p // 2 + 4, 4)

    def col_line(v, i):
        return line(xcol, v, v == 0, (0, 1, 3, 2)[i])

    def col_copies(v, i, src):
        step = 1 if v == 0 else 3
        return (send(src, col_line(v, i), cs.at[v, i, 0], cr.at[v, i], at(0, step, 0)),
                send(src, col_line(v, i), cs.at[v, i, 1], cr.at[v, i], at(0, 0, 0, 1)))

    def hop_of(v):
        return lag if v == 0 else lax.rem(4 - lag, 4)

    def col_root(v, i):
        @pl.when(jnp.logical_and(same, lag == 0))
        def _():
            src = line(xrow, q // 8 + 2 * v, v == 0, (0, 1, 3, 2)[i])
            for cp in col_copies(v, i, src):
                cp.start()
            pltpu.make_async_copy(src, col_line(v, i), loc.at[1 + 4 * v + i]).start()

    def col_relay(v, i, hop):
        @pl.when(jnp.logical_and(same, hop_of(v) == hop))
        def _():
            nxt, other = col_copies(v, i, col_line(v, i))
            other.wait_recv()
            if hop < 3:
                nxt.start()
            other.start()

    def col_end(v, i):
        nxt, other = col_copies(v, i, col_line(v, i))

        @pl.when(jnp.logical_not(same))
        def _():
            other.wait_recv()

        @pl.when(same)
        def _():
            other.wait_send()

        @pl.when(jnp.logical_and(same, hop_of(v) < 3))
        def _():
            nxt.wait_send()

        @pl.when(jnp.logical_and(same, lag == 0))
        def _():
            pltpu.make_async_copy(col_line(v, i), col_line(v, i), loc.at[1 + 4 * v + i]).wait()

    own.wait()
    c1.wait_recv()
    c0.wait_recv()
    acts = {"rs": row_start, "rw": row_wait, "cr": col_root, "cf": col_relay}

    def run(at_hook):
        for act in hooks.get(at_hook, ()):
            acts[act[0]](*act[1:])

    run("start")
    sub = lax.broadcasted_iota(jnp.int32, (8, 128), 0)
    for g in range(64):
        yy, cc, qq = g // 16, (g // 8) % 2, (2 * g) % 16
        for h in range(2):
            e, o = D[yy, cc, qq, h], D[yy, cc, qq + 1, h]
            M[8 * g:8 * g + 8, 256 * h:256 * h + 128] = jnp.where(sub < 4, e, pltpu.roll(o, 4, 0))
            M[8 * g:8 * g + 8, 256 * h + 128:256 * h + 256] = jnp.where(sub < 4, pltpu.roll(e, 4, 0), o)
    chol_body(M, T, U, run)
    inv[...] = M[...]
    lblk[...] = U[:, pl.ds(pl.multiple_of((p // 2) * 128, 128), 128)].T
    run("end")
    for v in range(2):
        for i in range(4):
            col_end(v, i)
    for cp in a0 + a1 + b0 + b1 + [c0, c1]:
        cp.wait_send()
    for u in range(4):
        for s in range(4):
            for cp in row[u][s]:
                cp.wait_send()


def default_hooks():
    h = {k: [] for k in ["start", "end"] + list(range(16))}
    U4 = range(4)
    h["start"] += [("rs", u, 0) for u in U4]
    h[2] += [a for u in U4 for a in (("rw", u, 0), ("rs", u, 1))]
    h[4] += [a for u in U4 for a in (("rw", u, 1), ("rs", u, 2))]
    h[4] += [("cr", v, 0) for v in range(2)]
    h[7] += [("cf", v, 0, 1) for v in range(2)]
    h[9] += [("cf", v, 0, 2) for v in range(2)]
    h[10] += [a for u in (0, 2) for a in (("rw", u, 2), ("rs", u, 3))]
    h[11] += [("cf", v, 0, 3) for v in range(2)]
    h[13] += [a for u in (1, 3) for a in (("rw", u, 2), ("rs", u, 3))]
    h[13] += [("cr", v, i) for i in (1, 2) for v in range(2)]
    h["end"] += [("cf", v, i, 1) for i in (1, 2) for v in range(2)]
    h["end"] += [("rw", u, 3) for u in U4]
    h["end"] += [("cr", v, 3) for v in range(2)]
    h["end"] += [("cf", v, i, 2) for i in (1, 2) for v in range(2)]
    h["end"] += [("cf", v, 3, 1) for v in range(2)]
    h["end"] += [("cf", v, i, 3) for i in (1, 2) for v in range(2)]
    h["end"] += [("cf", v, 3, 2) for v in range(2)]
    h["end"] += [("cf", v, 3, 3) for v in range(2)]
    return h


def gather_factor(d, panel):
    dma = pltpu.SemaphoreType.DMA
    anywhere = pl.BlockSpec(memory_space=pl.ANY)
    vmem = pl.BlockSpec(memory_space=pltpu.VMEM)
    return pl.pallas_call(
        functools.partial(gather_factor_kernel, default_hooks()),
        out_shape=[jax.ShapeDtypeStruct((512, 512), F32), jax.ShapeDtypeStruct((128, 512), F32),
                   jax.ShapeDtypeStruct((4, 4, 4, 32, 512), F32), jax.ShapeDtypeStruct((2, 4, 4, 32, 512), F32)],
        in_specs=[vmem, anywhere],
        out_specs=[vmem, vmem, anywhere, anywhere],
        scratch_shapes=[pltpu.VMEM((4, 2, 16, 2, 8, 128), F32), pltpu.VMEM((512, 512), F32), pltpu.VMEM((128, 256), F32),
                        pltpu.VMEM((512, 512), F32), dma((18,)), dma((18,)), dma((18,)), dma((18,)), dma((2,)), dma((2,)),
                        dma((4, 6)), dma((4, 6)), dma((2, 4, 2)), dma((2, 4)), dma((9,))],
        compiler_params=pltpu.CompilerParams(collective_id=0, has_side_effects=True, vmem_limit_bytes=40 << 20),
        name="gather_factor",
    )(d, panel)


def per_device(diag_block, panel, trailing):
    d = diag_block.reshape(4, 4, 128).transpose(1, 0, 2).reshape(2, 8, 128)
    inv, lblk, xrow, xcol = gather_factor(d, panel)
    c = trailing.reshape(4, 512, 2, 4, 128).transpose(0, 1, 3, 2, 4).reshape(16384, 128)
    factor_diag, factor_panel, out = update(inv, lblk, xcol.reshape(1024, 512), xrow.reshape(2048, 512), c)
    updated = out.reshape(4, 512, 4, 2, 128).transpose(0, 1, 3, 2, 4).reshape(4, 512, 2, 512)
    return factor_diag, factor_panel, updated


def solution(mesh):
    specs = (P(("prow", "pcol"), None), P(None, ("prow", "pcol"), None), P(None, "prow", None, "pcol"))
    return jax.shard_map(per_device, mesh=mesh, in_specs=specs, out_specs=specs, check_vma=False)
```

time: 176 us -> 91.3 us (0.52); the launches traced: 173 us -> 90.9 us
  waiting for transfers between devices: 76.2 us -> 0 us
  Pallas kernels: 40.9 us -> 86.7 us
  blocking collectives: 29.4 us -> 0 us
  between operations: 15.6 us -> 0.66 us
  local copies, waits for them, and re-layouts: 7.92 us -> 3.57 us
  other arithmetic: 3.13 us -> 0 us
    all_gather x3 -> x0, waiting for transfers between devices: 74.9 us -> none  [the longest x1 56.2 us: per_device(): row_blocks = lax.all_gather(panel, PCOL, axis=1, tiled=True)]
    pallas_call x2, Pallas kernels: 40.9 us -> 86.7 us  [the longest x1 68.4 us: gather_factor(): pl.pallas_call(functools.partial(gather_factor_kernel, default_hooks()),...]
    all_gather x3 -> x0, blocking collectives: 29.4 us -> none  [stacked_from(): blocks = lax.all_gather(blocks, axes[k])]
    select_n x1 -> x0, other arithmetic: 3.13 us -> none  [spread(): jnp.where(lax.axis_index(axis) == root, value, jnp.zeros_like(value))]
    transpose x2 -> x0, local copies, waits for them, and re-layouts: 2.42 us -> none  [the longest x1 1.35 us: stacked_from(): blocks = blocks.transpose(*back, *range(len(axes), blocks.ndim))]
    unnamed x7 -> x6, local copies, waits for them, and re-layouts: 4.15 us -> 3.57 us
  transfers between devices with their start and end apart: 4 -> 0, of which waited for: 2 -> 0; matrix products, arithmetic and copies ran while one was open for 3% -> 0% of each run, Pallas kernels for 13% -> 0%
where the time goes in v2:
time: 91.3 us; the launch traced here: 90.9 us
  Pallas kernels  86.7 us (95%)
  local copies, waits for them, and re-layouts  3.57 us (4%)
    pallas_call x1, Pallas kernels, gather_factor(): pl.pallas_call(functools.partial(gather_factor_kernel, default_hooks()),...  68.4 us
    pallas_call x1, Pallas kernels, update(): pl.pallas_call(update_kernel, grid=(8,), in_specs=[pl.BlockSpec((512, 512...  18.3 us
    unnamed x6, local copies, waits for them, and re-layouts  3.57 us

profile of v2, /device:TPU:9, one launch (start us, length us, event | category | flops | bytes accessed | tf_op | source)
XLA Modules:
  0.0 90.9 jit_solution(966306149373364823)
XLA Ops:
  0.6 0.0 copy-start.1
  0.6 0.9 %copy-done.1 = f32[4,32,512]{2,1,0:T(8,128)S(1)} copy-done((f32[4,32,512]{2,1,0:T(8,128)S(1)}, f32[4,32,512]{2,1,0:T(8,128)}, u32[]{:S(2)}) %copy-start.1) | copy-done | bytes 262168
  1.6 0.0 copy-start.2
  1.6 0.7 copy-done.2
  2.3 68.4 %gather_factor.1 = (f32[512,512]{1,0:T(8,128)S(1)}, f32[128,512]{1,0:T(8,128)S(1)}, f32[4,4,4,32,512]{4,3,2,1,0:T(8,128)S(1)}, f32[2,4,4,32,512]{4,3,2,1,0:T(8,128)S(1)}) custom-call(f32[2,8,128]{2,1,0:T(8,128)S(1)} %bitcast.19, f32[4,32,512]{2,1,0:T(8,128)S(1)} %copy-done.1), custom_call_target="tpu_custom_call" | custom-call | tf_op jit(solution)/shard_map/gather_factor/pallas_call | solution.py:369
  70.7 0.0 copy-start
  70.7 1.9 %copy-done = f32[4,4,4,32,512]{4,3,2,1,0:T(8,128)} copy-done((f32[4,4,4,32,512]{4,3,2,1,0:T(8,128)}, f32[4,4,4,32,512]{4,3,2,1,0:T(8,128)S(1)}, u32[]{:S(2)}) %copy-start) | copy-done | bytes 4194328
  72.6 18.3 %panel_update.1 = (f32[4,512]{1,0:T(4,128)}, f32[4,32,512]{2,1,0:T(8,128)}, f32[16384,128]{1,0:T(8,128)}) custom-call(f32[512,512]{1,0:T(8,128)S(1)} %get-tuple-element.10.inv, f32[128,512]{1,0:T(8,128)S(1)} %get-tuple-element.11.lblk, f32[1024,512]{1,0:T(8,128)S(1)} %bitcast.18, f32[2048,512]{1,0:T(8,128)} %bitcast.17, f32[16384,128]{1,0:T(8,128)} %bitcast.20), custom_call_target="tpu_custom_call" | custom-call | tf_op jit(solution)/shard_map/panel_update/pallas_call | solution.py:155
Async XLA Ops:
  0.6 1.0 %copy-start.1 = (f32[4,32,512]{2,1,0:T(8,128)S(1)}, f32[4,32,512]{2,1,0:T(8,128)}, u32[]{:S(2)}) copy-start(f32[4,32,512]{2,1,0:T(8,128)} %panel.1) | copy-start | bytes 786436
  1.6 0.7 copy-start.2
  70.7 1.9 %copy-start = (f32[4,4,4,32,512]{4,3,2,1,0:T(8,128)}, f32[4,4,4,32,512]{4,3,2,1,0:T(8,128)S(1)}, u32[]{:S(2)}) copy-start(f32[4,4,4,32,512]{4,3,2,1,0:T(8,128)S(1)} %get-tuple-element.13) | copy-start | bytes 12582916

commit v3 on v2

v3 whole, which is shorter than its diff:
```python
import functools

import jax
import jax.numpy as jnp
from jax import lax
from jax.experimental import pallas as pl
from jax.experimental.pallas import tpu as pltpu
from jax.sharding import PartitionSpec as P

F32 = jnp.float32
BF16 = jnp.bfloat16
HI = lax.Precision.HIGHEST
MESH = pl.DeviceIdType.MESH


def tdot(a, b, prec=HI):
    return lax.dot_general(a, b, (((0,), (0,)), ((), ())), precision=prec, preferred_element_type=F32)

def bc(col, n=128):
    return jnp.broadcast_to(col, (col.shape[0], n))

def elim8(G, c0, sub):
    n = len(G)
    C = [[bc(G[g][:, c0 + j:c0 + j + 1]) for j in range(8)] for g in range(n)]
    L = [G[g][:, :128] for g in range(n)]
    V = [G[g][:, 128:] for g in range(n)]
    dv = None
    for j in range(8):
        piv = [jnp.broadcast_to(C[0][l][j:j + 1, :], (8, 128)) for l in range(j, 8)]
        rinv = 1.0 / piv[0]
        rowL = jnp.broadcast_to(L[0][j:j + 1, :], (8, 128))
        rowV = jnp.broadcast_to(V[0][j:j + 1, :], (8, 128))
        dv = piv[0] if j == 0 else jnp.where(sub == j, piv[0], dv)
        for g in range(n):
            m = C[g][j] * rinv
            if g == 0:
                m = jnp.where(sub > j, m, 0.0)
            for l in range(j + 1, 8):
                C[g][l] = C[g][l] - m * piv[l - j]
            L[g] = L[g] - m * rowL
            V[g] = V[g] - m * rowV
    sc = lax.rsqrt(dv)
    L[0] = L[0] * sc
    V[0] = V[0] * sc
    return [jnp.concatenate([L[g], V[g]], 1) for g in range(n)]

def leaf(T, hook, k):
    sub = lax.broadcasted_iota(jnp.int32, (8, 128), 0)
    for sb in range(4):
        r0 = 32 * sb
        G = [T[r0 + 8 * g:r0 + 8 * g + 8, :] for g in range(4)]
        done = []
        for g in range(4):
            G = elim8(G, r0 + 8 * g, sub)
            done.append(G[0])
            T[r0 + 8 * g:r0 + 8 * g + 8, :] = G[0]
            G = G[1:]
        hook(4 * k + sb)
        if sb < 3:
            W = jnp.concatenate(done, 0)
            Pm = tdot(W[:, :128], W)
            T[r0 + 32:128, :] = T[r0 + 32:128, :] - Pm[r0 + 32:128, :]

def chol_body(M, T, U, hook, nb=4):
    row = lax.broadcasted_iota(jnp.int32, (128, 128), 0)
    col = lax.broadcasted_iota(jnp.int32, (128, 128), 1)
    eye = jnp.where(row == col, 1.0, 0.0).astype(F32)
    n = nb * 128
    for k in range(nb):
        a, b = k * 128, (k + 1) * 128
        T[:, :128] = M[a:b, a:b]
        T[:, 128:] = eye
        leaf(T, hook, k)
        Ukk = jnp.where(col >= row, T[:, :128], 0.0)
        Vkk = jnp.where(col <= row, T[:, 128:], 0.0)
        U[a:b, a:b] = Ukk
        if k > 0:
            U[a:b, :a] = jnp.zeros((128, a), F32)
            M[a:b, :a] = jnp.dot(Vkk, M[a:b, :a], precision=HI, preferred_element_type=F32)
        M[a:b, a:b] = Vkk
        if k < nb - 1:
            Ur = jnp.dot(Vkk, M[a:b, b:], precision=HI, preferred_element_type=F32)
            U[a:b, b:] = Ur
            M[a:b, b:] = jnp.zeros((128, n - b), F32)
            if k > 0:
                M[b:, :a] = M[b:, :a] - tdot(Ur, M[a:b, :a])
            M[b:, a:b] = -tdot(Ur, Vkk)
            M[b:, b:] = M[b:, b:] - tdot(Ur, Ur)


def halves(x):
    hi = x.astype(BF16)
    return hi, (x - hi.astype(F32)).astype(BF16)


def left3(x):
    hi, lo = halves(x)
    return jnp.concatenate([hi, hi, lo], 1)


def right3(x):
    hi, lo = halves(x)
    return jnp.concatenate([hi, lo, hi], 0)


def bdot(a, b):
    return jnp.dot(a, b, preferred_element_type=F32)


def solve_rows(x, l0, l1):
    return jnp.concatenate([bdot(left3(x[:, :256]), l0), bdot(left3(x), l1)], 1)


ROWS = 256


def update_kernel(inv, lblk, xcol, xrow, c, fdiag, fpan, out, l0, l1, cols, fs, made, sems):
    p, q = lax.axis_index("prow"), lax.axis_index("pcol")
    pair = lblk[pl.ds(pl.multiple_of((p % 2) * 64 + (q // 2) * 8, 8), 8), :]
    fdiag[...] = jnp.where(q % 2 == 0, pair[:4], pair[4:])
    l0[...] = right3(inv[:256, :256].T)
    l1[...] = right3(inv[256:, :].T)
    for k in range(4):
        f = solve_rows(xcol[256 * k:256 * (k + 1), :], l0[...], l1[...])
        cols[:, 256 * k:256 * (k + 1)] = right3(f.T)

    copies = []
    for u in range(4):
        f = solve_rows(xrow[512 * u:512 * (u + 1), :], l0[...], l1[...])
        fs[...] = f
        fpan[u] = fs[pl.ds(pl.multiple_of(q * 32, 32), 32), :]
        f3 = left3(f)

        def product(v, r):
            prod = bdot(f3[r:r + ROWS], cols[:, 512 * v:512 * (v + 1)])
            for t in range(4):
                at = pl.ds(8 * (512 * u + r) + 2 * t + v, ROWS, stride=8)
                made[at, :] = c[at, :] - prod[:, 128 * t:128 * (t + 1)]

        def keep(v, r):
            for t in range(4):
                at = pl.ds(8 * (512 * u + r) + 2 * t + v, ROWS, stride=8)
                made[at, :] = c[at, :]

        def both(v, r):
            present = v * 16 + q <= u * 8 + p
            pl.when(present)(functools.partial(product, v, r))
            pl.when(jnp.logical_not(present))(functools.partial(keep, v, r))

        for r in range(0, 512, ROWS):
            for v in range(2):
                if v == u // 2:
                    both(v, r)
                elif v < u // 2:
                    product(v, r)
                else:
                    keep(v, r)
            at = pl.ds(8 * (512 * u + r), 8 * ROWS)
            cp = pltpu.make_async_copy(made.at[at], out.at[at], sems.at[len(copies)])
            cp.start()
            copies.append(cp)
    for cp in copies:
        cp.wait()


def update(inv, lblk, xcol, xrow, c):
    vmem = pl.BlockSpec(memory_space=pltpu.VMEM)
    return pl.pallas_call(
        update_kernel,
        in_specs=[vmem] * 5,
        out_specs=[vmem, vmem, pl.BlockSpec(memory_space=pltpu.HBM)],
        out_shape=[jax.ShapeDtypeStruct((4, 512), F32), jax.ShapeDtypeStruct((4, 32, 512), F32),
                   jax.ShapeDtypeStruct((16384, 128), F32)],
        scratch_shapes=[pltpu.VMEM((768, 256), BF16), pltpu.VMEM((1536, 256), BF16), pltpu.VMEM((1536, 1024), BF16),
                        pltpu.VMEM((512, 512), F32), pltpu.VMEM((16384, 128), F32), pltpu.SemaphoreType.DMA((2048 // ROWS,))],
        compiler_params=pltpu.CompilerParams(vmem_limit_bytes=26 << 20),
        name="panel_update",
    )(inv, lblk, xcol, xrow, c)


def gather_factor_kernel(hooks, d, panel, inv, lblk, xrow, xcol, D, M, T, U, s1s, s1r, s2s, s2r, s3s, s3r, rs, rr, cs, cr, loc):
    p, q = lax.axis_index("prow"), lax.axis_index("pcol")
    y, c, x, z = p // 2, p % 2, q // 4, q % 4

    def at(dx, dy, dz, dc=0):
        return (lax.rem(y + dy, 4) * 2 + lax.rem(c + dc, 2), lax.rem(x + dx, 4) * 4 + lax.rem(z + dz, 4))

    def send(src, dst, ssem, rsem, dev):
        return pltpu.make_async_remote_copy(src_ref=src, dst_ref=dst, send_sem=ssem, recv_sem=rsem, device_id=dev, device_id_type=MESH)

    plane = [(dx, dz) for dx in range(4) for dz in range(4) if dx or dz]
    barrier = pltpu.get_barrier_semaphore()
    for dev in [at(dx, 0, dz) for dx, dz in plane] + [at(0, dy, 0) for dy in (1, 2, 3)] + [at(0, 0, 0, 1)]:
        pl.semaphore_signal(barrier, inc=1, device_id=dev, device_id_type=MESH)
    pl.semaphore_wait(barrier, 19)

    a0 = [send(d.at[0], D.at[0, y, c, q], s1s.at[k], s1r.at[k], at(dx, 0, dz)) for k, (dx, dz) in enumerate(plane)]
    a1 = [send(d.at[1], D.at[1, y, c, q], s1s.at[14 + dy], s1r.at[14 + dy], at(0, dy, 0)) for dy in (1, 2, 3)]
    for cp in a1 + a0:
        cp.start()
    dloc = pltpu.make_async_copy(d, D.at[:, y, c, q], loc.at[3])
    dloc.start()
    own = pltpu.make_async_copy(panel, xrow.at[:, :, x, z], loc.at[0])
    own.start()
    for cp in a1:
        cp.wait_recv()
    dloc.wait()
    b1 = [send(D.at[1, :, c, q], D.at[1, :, c, q], s2s.at[k], s2r.at[k], at(dx, 0, dz)) for k, (dx, dz) in enumerate(plane)]
    for cp in b1:
        cp.start()
    for cp in a0:
        cp.wait_recv()
    b0 = [send(D.at[0, y, c], D.at[0, y, c], s2s.at[14 + dy], s2r.at[14 + dy], at(0, dy, 0)) for dy in (1, 2, 3)]
    for cp in b0:
        cp.start()

    mate, away = 1 + 2 * lax.rem(x, 2), 3 - 2 * lax.rem(x, 2)
    first = x // 2

    def near(w, n):
        return at(0, 0, n) if w == 0 else at(n, 0, 0)

    def line(ref, w, off):
        if w == 0:
            return ref.at[lax.rem(x + off, 4)]
        return ref.at[:, lax.rem(z + off, 4)]

    ra = [send(panel.at[w], xrow.at[w, :, x, z], rs.at[3 * w + n - 1], rr.at[3 * w + n - 1], near(w, n)) for n in (1, 3, 2) for w in (0, 1)]

    def pick(w, n, k):
        u = lax.rem(x + n, 4) // 2 if w == 0 else first
        return xrow.at[w, u if k == 0 else 1 - u]

    rb, rc = {}, {}
    for w in (0, 1):
        for k in (0, 1):
            j = 6 + 3 * (2 * w + k)
            rb[w, k] = []
            for s, n in enumerate((1, 3)):
                ref = line(pick(w, n, k), w, 0)
                rb[w, k].append(send(ref, ref, rs.at[j + s], rr.at[j + s], at(n, 0, 0) if w == 0 else at(0, 0, n)))
            if w == 0:
                ref = line(xrow.at[0, first], 0, away if k == 0 else mate)
                rc[w, k] = send(ref, ref, rs.at[j + 2], rr.at[j + 2], at(mate if k == 0 else away, 0, 0))
            else:
                ref = line(xrow.at[1, first if k == 0 else 1 - first], 1, 3 if k == 0 else 1)
                rc[w, k] = send(ref, ref, rs.at[j + 2], rr.at[j + 2], at(0, 0, 1 if k == 0 else 3))

    lag = lax.rem(y - lax.rem(q, 8) // 2 + 4, 4)
    same = c == lax.rem(q, 2)
    is_root = p == lax.rem(q, 8)

    def chunk(ref, v, i):
        off, part = CHUNKS[i]
        ref = line(ref, v, off)
        return ref if part is None else ref.at[pl.ds(2 * part, 2)]

    def chain(src, v, i):
        part, spot = chunk(src, v, i), chunk(xcol.at[v], v, i)
        return (send(part, spot, cs.at[v, i, 0], cr.at[v, i], at(0, 1 if v == 0 else 3, 0)),
                send(part, spot, cs.at[v, i, 1], cr.at[v, i], at(0, 0, 0, 1)))

    def hop_of(v):
        return lag if v == 0 else lax.rem(4 - lag, 4)

    def col_root(*chunks):
        @pl.when(is_root)
        def _():
            both = [chain(xrow.at[v, first], v, i) for i in chunks for v in range(2)]
            for nxt, other in both:
                nxt.start()
            for nxt, other in both:
                other.start()

    def col_local():
        @pl.when(is_root)
        def _():
            for v in range(2):
                pltpu.make_async_copy(xrow.at[v, first], xcol.at[v], loc.at[1 + v]).start()

    def col_hop(i, hop):
        for v in range(2):
            @pl.when(jnp.logical_and(same, hop_of(v) == hop))
            def _():
                nxt, other = chain(xcol.at[v], v, i)
                other.wait_recv()
                if hop < 3:
                    nxt.start()
                other.start()

    def col_end():
        for v in range(2):
            for i in range(len(CHUNKS)):
                nxt, other = chain(xcol.at[v], v, i)
                pl.when(jnp.logical_not(same))(other.wait_recv)
                pl.when(same)(other.wait_send)
                pl.when(jnp.logical_and(same, hop_of(v) < 3))(nxt.wait_send)

            @pl.when(is_root)
            def _():
                pltpu.make_async_copy(xrow.at[v, first], xcol.at[v], loc.at[1 + v]).wait()

    def row_a_start():
        for cp in ra:
            cp.start()

    def row_a():
        for cp in ra:
            cp.wait_recv()
        for w in (0, 1):
            for cp in rb[w, 0]:
                cp.start()

    def row_b0():
        for w in (0, 1):
            for cp in rb[w, 0]:
                cp.wait_recv()
            rc[w, 0].start()
        rc[0, 1].start()
        for w in (0, 1):
            for cp in rb[w, 1]:
                cp.start()

    def row_c0():
        for w in (0, 1):
            rc[w, 0].wait_recv()

    def row_b1():
        for cp in rb[1, 1]:
            cp.wait_recv()
        rc[1, 1].start()

    def row_c1():
        for cp in rb[0, 1] + [rc[0, 1], rc[1, 1]]:
            cp.wait_recv()

    acts = {"as": row_a_start, "a": row_a, "b0": row_b0, "c0": row_c0, "b1": row_b1, "c1": row_c1,
            "root": col_root, "local": col_local, "hop": col_hop}

    def run(where):
        for act in hooks.get(where, ()):
            acts[act[0]](*act[1:])

    run("first")
    for cp in b1:
        cp.wait_recv()
    c1 = send(D.at[1, :, c], D.at[1, :, c], s3s.at[1], s3r.at[1], at(0, 0, 0, 1))
    c1.start()
    for cp in b0:
        cp.wait_recv()
    c0 = send(D.at[0, :, c], D.at[0, :, c], s3s.at[0], s3r.at[0], at(0, 0, 0, 1))
    c0.start()
    own.wait()
    run("second")
    c1.wait_recv()
    c0.wait_recv()
    run("start")
    sub = lax.broadcasted_iota(jnp.int32, (8, 128), 0)
    for g in range(64):
        yy, cc, qq = g // 16, (g // 8) % 2, (2 * g) % 16
        for h in range(2):
            e, o = D[h, yy, cc, qq], D[h, yy, cc, qq + 1]
            M[8 * g:8 * g + 8, 256 * h:256 * h + 128] = jnp.where(sub < 4, e, pltpu.roll(o, 4, 0))
            M[8 * g:8 * g + 8, 256 * h + 128:256 * h + 256] = jnp.where(sub < 4, pltpu.roll(e, 4, 0), o)
    chol_body(M, T, U, run)
    inv[...] = M[...]
    lblk[...] = U[:, pl.ds(pl.multiple_of((p // 2) * 128, 128), 128)].T
    run("end")
    col_end()
    for cp in a0 + a1 + b0 + b1 + [c0, c1] + ra + [cp for k in rb for cp in rb[k]] + list(rc.values()):
        cp.wait_send()


CHUNKS = ((0, None), (1, None), (3, None), (2, 0), (2, 1))


def default_hooks():
    return {
        "first": [("as",)],
        "second": [("a",), ("root", 0)],
        "start": [("hop", 0, 1)],
        0: [("b0",), ("root", 1, 2)],
        2: [("hop", 0, 2)],
        4: [("hop", 1, 1)],
        6: [("c0",), ("root", 3, 4), ("local",), ("hop", 2, 1), ("hop", 0, 3)],
        7: [("hop", 1, 2), ("b1",)],
        8: [("hop", 3, 1)],
        9: [("hop", 4, 1), ("hop", 2, 2)],
        11: [("hop", 3, 2), ("hop", 1, 3)],
        12: [("hop", 4, 2)],
        13: [("hop", 2, 3)],
        14: [("hop", 3, 3)],
        "end": [("hop", 4, 3), ("c1",)],
    }


def gather_factor(d, panel):
    dma = pltpu.SemaphoreType.DMA
    vmem = pl.BlockSpec(memory_space=pltpu.VMEM)
    return pl.pallas_call(
        functools.partial(gather_factor_kernel, default_hooks()),
        out_shape=[jax.ShapeDtypeStruct((512, 512), F32), jax.ShapeDtypeStruct((128, 512), F32),
                   jax.ShapeDtypeStruct((2, 2, 4, 4, 32, 512), F32), jax.ShapeDtypeStruct((2, 4, 4, 32, 512), F32)],
        in_specs=[pl.BlockSpec(memory_space=pl.ANY)] * 2,
        out_specs=[vmem] * 4,
        scratch_shapes=[pltpu.VMEM((2, 4, 2, 16, 8, 128), F32), pltpu.VMEM((512, 512), F32), pltpu.VMEM((128, 256), F32),
                        pltpu.VMEM((512, 512), F32), dma((18,)), dma((18,)), dma((18,)), dma((18,)), dma((2,)), dma((2,)),
                        dma((18,)), dma((18,)), dma((2, 5, 2)), dma((2, 5)), dma((4,))],
        compiler_params=pltpu.CompilerParams(collective_id=0, has_side_effects=True, vmem_limit_bytes=24 << 20),
        cost_estimate=pl.CostEstimate(flops=4 * 10**10, bytes_accessed=80 << 20, transcendentals=0),
        name="gather_factor",
    )(d, panel)


def per_device(diag_block, panel, trailing):
    d = diag_block.reshape(4, 4, 128).transpose(1, 0, 2).reshape(2, 8, 128)
    inv, lblk, xrow, xcol = gather_factor(d, panel.reshape(2, 2, 32, 512))
    c = trailing.reshape(4, 512, 2, 4, 128).transpose(0, 1, 3, 2, 4).reshape(16384, 128)
    factor_diag, factor_panel, out = update(inv, lblk, xcol.reshape(1024, 512), xrow.reshape(2048, 512), c)
    updated = out.reshape(4, 512, 4, 2, 128).transpose(0, 1, 3, 2, 4).reshape(4, 512, 2, 512)
    return factor_diag, factor_panel, updated


def solution(mesh):
    specs = (P(("prow", "pcol"), None), P(None, ("prow", "pcol"), None), P(None, "prow", None, "pcol"))
    return jax.shard_map(per_device, mesh=mesh, in_specs=specs, out_specs=specs, check_vma=False)
```

time: 91.3 us -> 74 us (0.81)
  Pallas kernels: 86.7 us -> 71.3 us
  local copies, waits for them, and re-layouts: 3.57 us -> 1.64 us
    pallas_call x1, Pallas kernels: 68.4 us -> 55.4 us  [gather_factor(): pl.pallas_call(functools.partial(gather_factor_kernel, default_hooks()),...]
    pallas_call x1, Pallas kernels: 18.3 us -> 16 us  [update(): pl.pallas_call(update_kernel, in_specs=[vmem] * 5, out_specs=[vmem, vmem,...]
    unnamed x6, local copies, waits for them, and re-layouts: 3.57 us -> 1.64 us
where the time goes in v3:
time: 74 us; the launch traced here: 73.8 us
  Pallas kernels  71.3 us (96%)
  local copies, waits for them, and re-layouts  1.64 us (2%)
  between operations  0.84 us (1%)
    pallas_call x1, Pallas kernels, gather_factor(): pl.pallas_call(functools.partial(gather_factor_kernel, default_hooks()),...  55.4 us
    pallas_call x1, Pallas kernels, update(): pl.pallas_call(update_kernel, in_specs=[vmem] * 5, out_specs=[vmem, vmem,...  16 us
    unnamed x6, local copies, waits for them, and re-layouts  1.64 us

profile of v3, /device:TPU:9, one launch (start us, length us, event | category | flops | bytes accessed | tf_op | source)
XLA Modules:
  0.0 73.8 jit_solution(1535690433559593501)
XLA Ops:
  0.6 0.0 copy-start.1
  0.6 0.9 %copy-done.1 = f32[4,32,512]{2,1,0:T(8,128)S(1)} copy-done((f32[4,32,512]{2,1,0:T(8,128)S(1)}, f32[4,32,512]{2,1,0:T(8,128)}, u32[]{:S(2)}) %copy-start.1) | copy-done | bytes 262168
  1.6 0.0 copy-start.2
  1.6 0.7 copy-done.2
  2.3 0.0 copy-start
  2.3 55.4 %gather_factor.1 = (f32[512,512]{1,0:T(8,128)S(1)}, f32[128,512]{1,0:T(8,128)S(1)}, f32[2,2,4,4,32,512]{5,4,3,2,1,0:T(8,128)S(1)}, f32[2,4,4,32,512]{4,3,2,1,0:T(8,128)S(1)}) custom-call(f32[2,8,128]{2,1,0:T(8,128)S(1)} %bitcast.22, f32[2,2,32,512]{3,2,1,0:T(8,128)S(1)} %bitcast.21), custom_call_target="tpu_custom_call" | custom-call | flops 40000000000 | bytes 83886080 | tf_op jit(solution)/shard_map/gather_factor/pallas_call | solution.py:400
  57.6 0.0 copy-done
  57.6 16.0 %panel_update.1 = (f32[4,512]{1,0:T(4,128)}, f32[4,32,512]{2,1,0:T(8,128)}, f32[16384,128]{1,0:T(8,128)}) custom-call(f32[512,512]{1,0:T(8,128)S(1)} %get-tuple-element.10.inv, f32[128,512]{1,0:T(8,128)S(1)} %get-tuple-element.11.lblk, f32[1024,512]{1,0:T(8,128)S(1)} %bitcast.20, f32[2048,512]{1,0:T(8,128)S(1)} %bitcast.19, f32[16384,128]{1,0:T(8,128)S(1)} %bitcast.18), custom_call_target="tpu_custom_call" | custom-call | tf_op jit(solution)/shard_map/panel_update/pallas_call | solution.py:168
Async XLA Ops:
  0.6 1.0 %copy-start.1 = (f32[4,32,512]{2,1,0:T(8,128)S(1)}, f32[4,32,512]{2,1,0:T(8,128)}, u32[]{:S(2)}) copy-start(f32[4,32,512]{2,1,0:T(8,128)} %param.4) | copy-start | bytes 786436
  1.6 0.7 copy-start.2
  2.3 55.4 %copy-start = (f32[4,512,2,512]{3,2,1,0:T(2,128)S(1)}, f32[4,512,2,512]{3,2,1,0:T(2,128)}, u32[]{:S(2)}) copy-start(f32[4,512,2,512]{3,2,1,0:T(2,128)} %param.5) | copy-start | bytes 25165828

commit v4 on v3

--- a/solution.py
+++ b/solution.py
@@ -114,22 +114,18 @@
 ROWS = 256
 
 
-def update_kernel(inv, lblk, xcol, xrow, c, fdiag, fpan, out, l0, l1, cols, fs, made, sems):
+def update_kernel(lblk, l0, l1, fhi, flo, frows, xcol, c, fdiag, fpan, out, cols, made, sems):
     p, q = lax.axis_index("prow"), lax.axis_index("pcol")
     pair = lblk[pl.ds(pl.multiple_of((p % 2) * 64 + (q // 2) * 8, 8), 8), :]
     fdiag[...] = jnp.where(q % 2 == 0, pair[:4], pair[4:])
-    l0[...] = right3(inv[:256, :256].T)
-    l1[...] = right3(inv[256:, :].T)
+    fpan[...] = frows[...]
     for k in range(4):
         f = solve_rows(xcol[256 * k:256 * (k + 1), :], l0[...], l1[...])
         cols[:, 256 * k:256 * (k + 1)] = right3(f.T)
 
     copies = []
     for u in range(4):
-        f = solve_rows(xrow[512 * u:512 * (u + 1), :], l0[...], l1[...])
-        fs[...] = f
-        fpan[u] = fs[pl.ds(pl.multiple_of(q * 32, 32), 32), :]
-        f3 = left3(f)
+        f3 = jnp.concatenate([fhi[u], fhi[u], flo[u]], 1)
 
         def product(v, r):
             prod = bdot(f3[r:r + ROWS], cols[:, 512 * v:512 * (v + 1)])
@@ -163,22 +159,21 @@
         cp.wait()
 
 
-def update(inv, lblk, xcol, xrow, c):
+def update(lblk, l0, l1, fhi, flo, frows, xcol, c):
     vmem = pl.BlockSpec(memory_space=pltpu.VMEM)
     return pl.pallas_call(
         update_kernel,
-        in_specs=[vmem] * 5,
+        in_specs=[vmem] * 8,
         out_specs=[vmem, vmem, pl.BlockSpec(memory_space=pltpu.HBM)],
         out_shape=[jax.ShapeDtypeStruct((4, 512), F32), jax.ShapeDtypeStruct((4, 32, 512), F32),
                    jax.ShapeDtypeStruct((16384, 128), F32)],
-        scratch_shapes=[pltpu.VMEM((768, 256), BF16), pltpu.VMEM((1536, 256), BF16), pltpu.VMEM((1536, 1024), BF16),
-                        pltpu.VMEM((512, 512), F32), pltpu.VMEM((16384, 128), F32), pltpu.SemaphoreType.DMA((2048 // ROWS,))],
+        scratch_shapes=[pltpu.VMEM((1536, 1024), BF16), pltpu.VMEM((16384, 128), F32), pltpu.SemaphoreType.DMA((2048 // ROWS,))],
         compiler_params=pltpu.CompilerParams(vmem_limit_bytes=26 << 20),
         name="panel_update",
-    )(inv, lblk, xcol, xrow, c)
-
-
-def gather_factor_kernel(hooks, d, panel, inv, lblk, xrow, xcol, D, M, T, U, s1s, s1r, s2s, s2r, s3s, s3r, rs, rr, cs, cr, loc):
+    )(lblk, l0, l1, fhi, flo, frows, xcol, c)
+
+
+def gather_factor_kernel(hooks, d, panel, lblk, l0, l1, fhi, flo, fpan, xcol, xrow, fs, D, M, T, U, s1s, s1r, s2s, s2r, s3s, s3r, rs, rr, cs, cr, loc):
     p, q = lax.axis_index("prow"), lax.axis_index("pcol")
     y, c, x, z = p // 2, p % 2, q // 4, q % 4
 
@@ -214,8 +209,14 @@
     for cp in b0:
         cp.start()
 
-    mate, away = 1 + 2 * lax.rem(x, 2), 3 - 2 * lax.rem(x, 2)
     first = x // 2
+
+    def place(w):
+        return x if w == 0 else z
+
+    def prior(w, n):
+        there = lax.rem(place(w) + n, 4) // 2
+        return there if w == 0 else lax.rem(first + there + lax.rem(p, 4) // 2, 2)
 
     def near(w, n):
         return at(0, 0, n) if w == 0 else at(n, 0, 0)
@@ -228,23 +229,23 @@
     ra = [send(panel.at[w], xrow.at[w, :, x, z], rs.at[3 * w + n - 1], rr.at[3 * w + n - 1], near(w, n)) for n in (1, 3, 2) for w in (0, 1)]
 
     def pick(w, n, k):
-        u = lax.rem(x + n, 4) // 2 if w == 0 else first
+        u = prior(w, n)
         return xrow.at[w, u if k == 0 else 1 - u]
+
+    def along(w, n):
+        return at(n, 0, 0) if w == 0 else at(0, 0, n)
 
     rb, rc = {}, {}
     for w in (0, 1):
+        mate, away = 1 + 2 * lax.rem(place(w), 2), 3 - 2 * lax.rem(place(w), 2)
         for k in (0, 1):
             j = 6 + 3 * (2 * w + k)
             rb[w, k] = []
             for s, n in enumerate((1, 3)):
                 ref = line(pick(w, n, k), w, 0)
-                rb[w, k].append(send(ref, ref, rs.at[j + s], rr.at[j + s], at(n, 0, 0) if w == 0 else at(0, 0, n)))
-            if w == 0:
-                ref = line(xrow.at[0, first], 0, away if k == 0 else mate)
-                rc[w, k] = send(ref, ref, rs.at[j + 2], rr.at[j + 2], at(mate if k == 0 else away, 0, 0))
-            else:
-                ref = line(xrow.at[1, first if k == 0 else 1 - first], 1, 3 if k == 0 else 1)
-                rc[w, k] = send(ref, ref, rs.at[j + 2], rr.at[j + 2], at(0, 0, 1 if k == 0 else 3))
+                rb[w, k].append(send(ref, ref, rs.at[j + s], rr.at[j + s], along(w, n)))
+            ref = line(pick(w, 0, 0), w, away if k == 0 else mate)
+            rc[w, k] = send(ref, ref, rs.at[j + 2], rr.at[j + 2], along(w, mate if k == 0 else away))
 
     lag = lax.rem(y - lax.rem(q, 8) // 2 + 4, 4)
     same = c == lax.rem(q, 2)
@@ -316,8 +317,10 @@
             for cp in rb[w, 0]:
                 cp.wait_recv()
             rc[w, 0].start()
-        rc[0, 1].start()
+
+    def row_b1():
         for w in (0, 1):
+            rc[w, 1].start()
             for cp in rb[w, 1]:
                 cp.start()
 
@@ -325,17 +328,20 @@
         for w in (0, 1):
             rc[w, 0].wait_recv()
 
-    def row_b1():
-        for cp in rb[1, 1]:
-            cp.wait_recv()
-        rc[1, 1].start()
-
     def row_c1():
-        for cp in rb[0, 1] + [rc[0, 1], rc[1, 1]]:
-            cp.wait_recv()
+        for w in (0, 1):
+            for cp in rb[w, 1] + [rc[w, 1]]:
+                cp.wait_recv()
+
+    def solve(w, k):
+        u = prior(w, 0) if k == 0 else 1 - prior(w, 0)
+        f = solve_rows(xrow[w, u].reshape(512, 512), l0[...], l1[...])
+        fs[...] = f
+        fpan[2 * w + u] = fs[pl.ds(pl.multiple_of(q * 32, 32), 32), :]
+        fhi[2 * w + u], flo[2 * w + u] = halves(f)
 
     acts = {"as": row_a_start, "a": row_a, "b0": row_b0, "c0": row_c0, "b1": row_b1, "c1": row_c1,
-            "root": col_root, "local": col_local, "hop": col_hop}
+            "root": col_root, "local": col_local, "hop": col_hop, "f": solve}
 
     def run(where):
         for act in hooks.get(where, ()):
@@ -363,7 +369,8 @@
             M[8 * g:8 * g + 8, 256 * h:256 * h + 128] = jnp.where(sub < 4, e, pltpu.roll(o, 4, 0))
             M[8 * g:8 * g + 8, 256 * h + 128:256 * h + 256] = jnp.where(sub < 4, pltpu.roll(e, 4, 0), o)
     chol_body(M, T, U, run)
-    inv[...] = M[...]
+    l0[...] = right3(M[:256, :256].T)
+    l1[...] = right3(M[256:, :].T)
     lblk[...] = U[:, pl.ds(pl.multiple_of((p // 2) * 128, 128), 128)].T
     run("end")
     col_end()
@@ -379,18 +386,18 @@
         "first": [("as",)],
         "second": [("a",), ("root", 0)],
         "start": [("hop", 0, 1)],
-        0: [("b0",), ("root", 1, 2)],
+        0: [("b0",), ("root", 1, 2), ("b1",)],
         2: [("hop", 0, 2)],
         4: [("hop", 1, 1)],
-        6: [("c0",), ("root", 3, 4), ("local",), ("hop", 2, 1), ("hop", 0, 3)],
-        7: [("hop", 1, 2), ("b1",)],
+        6: [("hop", 2, 1), ("hop", 0, 3)],
+        7: [("c0",), ("root", 3, 4), ("local",), ("hop", 1, 2)],
         8: [("hop", 3, 1)],
         9: [("hop", 4, 1), ("hop", 2, 2)],
         11: [("hop", 3, 2), ("hop", 1, 3)],
         12: [("hop", 4, 2)],
         13: [("hop", 2, 3)],
         14: [("hop", 3, 3)],
-        "end": [("hop", 4, 3), ("c1",)],
+        "end": [("f", 0, 0), ("f", 1, 0), ("hop", 4, 3), ("c1",), ("f", 0, 1), ("f", 1, 1)],
     }
 
 
@@ -399,11 +406,12 @@
     vmem = pl.BlockSpec(memory_space=pltpu.VMEM)
     return pl.pallas_call(
         functools.partial(gather_factor_kernel, default_hooks()),
-        out_shape=[jax.ShapeDtypeStruct((512, 512), F32), jax.ShapeDtypeStruct((128, 512), F32),
-                   jax.ShapeDtypeStruct((2, 2, 4, 4, 32, 512), F32), jax.ShapeDtypeStruct((2, 4, 4, 32, 512), F32)],
+        out_shape=[jax.ShapeDtypeStruct((128, 512), F32), jax.ShapeDtypeStruct((768, 256), BF16), jax.ShapeDtypeStruct((1536, 256), BF16),
+                   jax.ShapeDtypeStruct((4, 512, 512), BF16), jax.ShapeDtypeStruct((4, 512, 512), BF16),
+                   jax.ShapeDtypeStruct((4, 32, 512), F32), jax.ShapeDtypeStruct((2, 4, 4, 32, 512), F32)],
         in_specs=[pl.BlockSpec(memory_space=pl.ANY)] * 2,
-        out_specs=[vmem] * 4,
-        scratch_shapes=[pltpu.VMEM((2, 4, 2, 16, 8, 128), F32), pltpu.VMEM((512, 512), F32), pltpu.VMEM((128, 256), F32),
+        out_specs=[vmem] * 7,
+        scratch_shapes=[pltpu.VMEM((2, 2, 4, 4, 32, 512), F32), pltpu.VMEM((512, 512), F32), pltpu.VMEM((2, 4, 2, 16, 8, 128), F32), pltpu.VMEM((512, 512), F32), pltpu.VMEM((128, 256), F32),
                         pltpu.VMEM((512, 512), F32), dma((18,)), dma((18,)), dma((18,)), dma((18,)), dma((2,)), dma((2,)),
                         dma((18,)), dma((18,)), dma((2, 5, 2)), dma((2, 5)), dma((4,))],
         compiler_params=pltpu.CompilerParams(collective_id=0, has_side_effects=True, vmem_limit_bytes=24 << 20),
@@ -414,9 +422,9 @@
 
 def per_device(diag_block, panel, trailing):
     d = diag_block.reshape(4, 4, 128).transpose(1, 0, 2).reshape(2, 8, 128)
-    inv, lblk, xrow, xcol = gather_factor(d, panel.reshape(2, 2, 32, 512))
+    lblk, l0, l1, fhi, flo, fpan, xcol = gather_factor(d, panel.reshape(2, 2, 32, 512))
     c = trailing.reshape(4, 512, 2, 4, 128).transpose(0, 1, 3, 2, 4).reshape(16384, 128)
-    factor_diag, factor_panel, out = update(inv, lblk, xcol.reshape(1024, 512), xrow.reshape(2048, 512), c)
+    factor_diag, factor_panel, out = update(lblk, l0, l1, fhi, flo, fpan, xcol.reshape(1024, 512), c)
     updated = out.reshape(4, 512, 4, 2, 128).transpose(0, 1, 3, 2, 4).reshape(4, 512, 2, 512)
     return factor_diag, factor_panel, updated
 

time: 74 us -> 70.6 us (0.954)
  Pallas kernels: 71.3 us -> 67.5 us
    pallas_call x1, Pallas kernels: 16 us -> 12.1 us  [update(): pl.pallas_call(update_kernel, in_specs=[vmem] * 8, out_specs=[vmem, vmem,...]
    unnamed x6 -> x8, local copies, waits for them, and re-layouts: 1.64 us -> 2.03 us
where the time goes in v4:
time: 70.6 us; the launch traced here: 70.4 us
  Pallas kernels  67.5 us (96%)
  local copies, waits for them, and re-layouts  2.03 us (3%)
  between operations  0.86 us (1%)
    pallas_call x1, Pallas kernels, gather_factor(): pl.pallas_call(functools.partial(gather_factor_kernel, default_hooks()),...  55.3 us
    pallas_call x1, Pallas kernels, update(): pl.pallas_call(update_kernel, in_specs=[vmem] * 8, out_specs=[vmem, vmem,...  12.1 us
    unnamed x8, local copies, waits for them, and re-layouts  2.03 us

profile of v4, /device:TPU:9, one launch (start us, length us, event | category | flops | bytes accessed | tf_op | source)
XLA Modules:
  0.0 70.4 jit_solution(17568917259518044838)
XLA Ops:
  0.6 0.0 slice-start
  0.6 0.0 copy-start
  0.7 1.1 %copy-done = f32[4,32,512]{2,1,0:T(8,128)S(1)} copy-done((f32[4,32,512]{2,1,0:T(8,128)S(1)}, f32[4,32,512]{2,1,0:T(8,128)}, u32[]{:S(2)}) %copy-start) | copy-done | bytes 262168
  1.7 0.0 copy-start.1
  1.7 0.9 %copy-done.1 = f32[4,512]{1,0:T(4,128)S(1)} copy-done((f32[4,512]{1,0:T(4,128)S(1)}, f32[4,512]{1,0:T(4,128)}, u32[]{:S(2)}) %copy-start.1) | copy-done | bytes 8216
  2.7 0.0 slice-start.1
  2.7 55.3 %gather_factor.1 = (f32[128,512]{1,0:T(8,128)S(1)}, bf16[768,256]{1,0:T(8,128)(2,1)S(1)}, bf16[1536,256]{1,0:T(8,128)(2,1)S(1)}, bf16[4,512,512]{2,1,0:T(8,128)(...) custom-call(f32[2,8,128]{2,1,0:T(8,128)S(1)} %bitcast.22, ...), custom_call_target="tpu_custom_call" | custom-call | flops 40000000000 | bytes 83886080 | tf_op jit(solution)/shard_map/gather_factor/pallas_call | solution.py:407
  58.0 0.0 slice-done
  58.0 0.0 slice-done.1
  58.0 12.1 %panel_update.1 = (f32[4,512]{1,0:T(4,128)}, f32[4,32,512]{2,1,0:T(8,128)}, f32[16384,128]{1,0:T(8,128)}) custom-call(f32[128,512]{1,0:T(8,128)S(1)} %get-tuple-element.13.lblk, bf16[768,256]{1,0:T(8,128)(2,1)S(1)} %get-tuple-element.14.l0, bf16[1536,256]{1,0:T(8,128)(2,1)S(1)} %get-tuple-element.15.l1, bf16[4,512,512]{2,1,0:T(8,128)(2,1)S(1)} %get-tuple-element.16.fhi, ...), custom_call_target="tpu_custom_call" | custom-call | tf_op jit(solution)/shard_map/panel_update/pallas_call | solution.py:164
  (1 shorter events, 0.0 us)
Async XLA Ops:
  0.6 57.4 %slice-start = ((s8[8388608]{0:T(1024)(128)(4,1)}), s8[4194304]{0:T(1024)(128)(4,1)S(1)}, s32[]{:S(2)}) async-start(s8[8388608]{0:T(1024)(128)(4,1)} %bitcast.17), calls=%async_computation | async-start | bytes 8388608
  0.6 1.1 %copy-start = (f32[4,32,512]{2,1,0:T(8,128)S(1)}, f32[4,32,512]{2,1,0:T(8,128)}, u32[]{:S(2)}) copy-start(f32[4,32,512]{2,1,0:T(8,128)} %param.4) | copy-start | bytes 786436
  1.7 0.9 %copy-start.1 = (f32[4,512]{1,0:T(4,128)S(1)}, f32[4,512]{1,0:T(4,128)}, u32[]{:S(2)}) copy-start(f32[4,512]{1,0:T(4,128)} %param.3) | copy-start | bytes 24580
  2.7 55.4 %slice-start.1 = ((s8[8388608]{0:T(1024)(128)(4,1)}), s8[4194304]{0:T(1024)(128)(4,1)S(1)}, s32[]{:S(2)}) async-start(s8[8388608]{0:T(1024)(128)(4,1)} %bitcast.17), calls=%async_computation.1 | async-start | bytes 8388608

commit v5 on v4

--- a/solution.py
+++ b/solution.py
@@ -111,7 +111,7 @@
     return jnp.concatenate([bdot(left3(x[:, :256]), l0), bdot(left3(x), l1)], 1)
 
 
-ROWS = 256
+ROWS = 128
 
 
 def update_kernel(lblk, l0, l1, fhi, flo, frows, xcol, c, fdiag, fpan, out, cols, made, sems):

time: 70.6 us -> 72.7 us (1.030)
  Pallas kernels: 67.5 us -> 69.5 us
    pallas_call x1, Pallas kernels: 12.1 us -> 14.2 us  [update(): pl.pallas_call(update_kernel, in_specs=[vmem] * 8, out_specs=[vmem, vmem,...]
where the time goes in v5:
time: 72.7 us; the launch traced here: 72.4 us
  Pallas kernels  69.5 us (96%)
  local copies, waits for them, and re-layouts  2.03 us (3%)
  between operations  0.86 us (1%)
    pallas_call x1, Pallas kernels, gather_factor(): pl.pallas_call(functools.partial(gather_factor_kernel, default_hooks()),...  55.3 us
    pallas_call x1, Pallas kernels, update(): pl.pallas_call(update_kernel, in_specs=[vmem] * 8, out_specs=[vmem, vmem,...  14.2 us
    unnamed x8, local copies, waits for them, and re-layouts  2.03 us

profile of v5, /device:TPU:9, one launch (start us, length us, event | category | flops | bytes accessed | tf_op | source)
XLA Modules:
  0.0 72.4 jit_solution(17630610931204308133)
XLA Ops:
  0.6 0.0 slice-start
  0.6 0.0 copy-start
  0.7 1.1 %copy-done = f32[4,32,512]{2,1,0:T(8,128)S(1)} copy-done((f32[4,32,512]{2,1,0:T(8,128)S(1)}, f32[4,32,512]{2,1,0:T(8,128)}, u32[]{:S(2)}) %copy-start) | copy-done | bytes 262168
  1.7 0.0 copy-start.1
  1.7 0.9 %copy-done.1 = f32[4,512]{1,0:T(4,128)S(1)} copy-done((f32[4,512]{1,0:T(4,128)S(1)}, f32[4,512]{1,0:T(4,128)}, u32[]{:S(2)}) %copy-start.1) | copy-done | bytes 8216
  2.7 0.0 slice-start.1
  2.7 55.3 %gather_factor.1 = (f32[128,512]{1,0:T(8,128)S(1)}, bf16[768,256]{1,0:T(8,128)(2,1)S(1)}, bf16[1536,256]{1,0:T(8,128)(2,1)S(1)}, bf16[4,512,512]{2,1,0:T(8,128)(...) custom-call(f32[2,8,128]{2,1,0:T(8,128)S(1)} %bitcast.22, ...), custom_call_target="tpu_custom_call" | custom-call | flops 40000000000 | bytes 83886080 | tf_op jit(solution)/shard_map/gather_factor/pallas_call | solution.py:407
  58.0 0.0 slice-done
  58.0 0.0 slice-done.1
  58.0 14.2 %panel_update.1 = (f32[4,512]{1,0:T(4,128)}, f32[4,32,512]{2,1,0:T(8,128)}, f32[16384,128]{1,0:T(8,128)}) custom-call(f32[128,512]{1,0:T(8,128)S(1)} %get-tuple-element.13.lblk, bf16[768,256]{1,0:T(8,128)(2,1)S(1)} %get-tuple-element.14.l0, bf16[1536,256]{1,0:T(8,128)(2,1)S(1)} %get-tuple-element.15.l1, bf16[4,512,512]{2,1,0:T(8,128)(2,1)S(1)} %get-tuple-element.16.fhi, ...), custom_call_target="tpu_custom_call" | custom-call | tf_op jit(solution)/shard_map/panel_update/pallas_call | solution.py:164
  (1 shorter events, 0.0 us)
Async XLA Ops:
  0.6 57.4 %slice-start = ((s8[8388608]{0:T(1024)(128)(4,1)}), s8[4194304]{0:T(1024)(128)(4,1)S(1)}, s32[]{:S(2)}) async-start(s8[8388608]{0:T(1024)(128)(4,1)} %bitcast.17), calls=%async_computation | async-start | bytes 8388608
  0.6 1.1 %copy-start = (f32[4,32,512]{2,1,0:T(8,128)S(1)}, f32[4,32,512]{2,1,0:T(8,128)}, u32[]{:S(2)}) copy-start(f32[4,32,512]{2,1,0:T(8,128)} %param.4) | copy-start | bytes 786436
  1.7 0.9 %copy-start.1 = (f32[4,512]{1,0:T(4,128)S(1)}, f32[4,512]{1,0:T(4,128)}, u32[]{:S(2)}) copy-start(f32[4,512]{1,0:T(4,128)} %param.3) | copy-start | bytes 24580
  2.7 55.4 %slice-start.1 = ((s8[8388608]{0:T(1024)(128)(4,1)}), s8[4194304]{0:T(1024)(128)(4,1)S(1)}, s32[]{:S(2)}) async-start(s8[8388608]{0:T(1024)(128)(4,1)} %bitcast.17), calls=%async_computation.1 | async-start | bytes 8388608
